TPU v7x, 256 devices: a whole 4x4x8 slice. The times are simulated.
256 devices in a mesh: leaf: 256 (over z, x, y, core).
Axes of the slice: x: 4, y: 4, z: 8, core: 2. Of those that a mesh axis runs over, the one named last changes fastest.
Arguments:
- coords: float32 [3, 131072], P(None, 'leaf'), may hold values from 0 to 2
- latent: float32 [131072], P('leaf'), may hold values from -3 to 3
- labels: int32 [131072], P('leaf'), may hold values from 0 to 1
- site_order: int32 [256, 512], P('leaf'), may hold values from 0 to 511, each once within a row
- level_bases: bfloat16 [4, 256, 131072], P(None, None, 'leaf'), may hold values from -0.75 to 0.75
Outputs:
- solution: float32 [131072], P('leaf')
Inputs may be any that keep to these rules, and one draw needn't show every extreme that they name: Each row of site_order is a permutation of 0 to 511.
All inputs are finite; a program needn't handle non-finite values.
Results may differ from a plain program's by a relative error of at most 0.0003.
Values sent between devices are 32-bit elements; how exact they have to be, the bound alone decides.
A program may use at most 64 MiB of HBM per device.

v0:
```python
import math

import jax
import jax.numpy as jnp
from jax import lax
from jax.sharding import PartitionSpec as P

length_scale = 0.25
signal_variance = 16.0
root_five = math.sqrt(5.0)
highest = lax.Precision.HIGHEST


def from_partner(value, axis, bit):
    mask = 2**bit
    pairs = [(source, source ^ mask) for source in range(lax.axis_size(axis))]
    return lax.ppermute(value, axis, pairs)


def leaf_solve(coords, latent, labels, site_order, level_bases):
    tree_latent = jnp.take(latent, site_order)
    tree_target = jnp.take(labels, site_order).astype(jnp.float32)
    probability = jax.nn.sigmoid(tree_latent)
    weight = probability * (1.0 - probability)
    root_weight = jnp.sqrt(weight)
    right_side = root_weight * (weight * tree_latent + tree_target - probability)
    differences = coords[:, :, None] - coords[:, None, :]
    distance = jnp.sqrt(jnp.sum(differences * differences, axis=0))
    scaled = root_five * distance / length_scale
    kernel = signal_variance * (1.0 + scaled + scaled * scaled / 3.0) * jnp.exp(-scaled)
    site_count = tree_latent.shape[0]
    leaf_matrix = (
        jnp.eye(site_count, dtype=jnp.float32)
        + root_weight[:, None] * kernel * root_weight[None, :]
    )
    factor = jnp.linalg.cholesky(leaf_matrix)
    scaled_bases = level_bases.astype(jnp.float32) * root_weight[None, None, :]
    stacked = jnp.concatenate([scaled_bases.reshape(-1, site_count).T, right_side[:, None]], axis=1)
    solved = jax.scipy.linalg.cho_solve((factor, True), stacked)
    applied = solved[:, :-1].T.reshape(scaled_bases.shape)
    return (scaled_bases, applied, solved[:, -1])


def node_terms(level_basis, applied, vector):
    gram_terms = jnp.einsum("rm,jsm->jrs", level_basis, applied, precision=highest)
    projection = jnp.dot(level_basis, vector, precision=highest)
    return (gram_terms, projection)


def core_solve(gram_terms, projection):
    rank_size = gram_terms.shape[1]
    remaining = gram_terms.shape[0] - 1
    core_matrix = jnp.eye(rank_size, dtype=jnp.float32) + gram_terms[0]
    core_factor = jnp.linalg.cholesky(core_matrix)
    right_hand = jnp.concatenate(
        [
            jnp.transpose(gram_terms[1:], (1, 0, 2)).reshape(rank_size, remaining * rank_size),
            projection[:, None],
        ],
        axis=1,
    )
    solution = jax.scipy.linalg.cho_solve((core_factor, True), right_hand)
    coefficients = jnp.transpose(
        solution[:, : remaining * rank_size].reshape(rank_size, remaining, rank_size), (1, 0, 2)
    )
    return (coefficients, solution[:, -1])


def apply_update(applied, vector, coefficients, coeff_vector):
    current_cols = applied[0]
    remaining_cols = applied[1:] - jnp.einsum(
        "jrs,rm->jsm", coefficients, current_cols, precision=highest
    )
    vector = vector - jnp.dot(coeff_vector, current_cols, precision=highest)
    return (remaining_cols, vector)


def node_sum_whole(gram_terms, projection, depth):
    for bit_index in range(depth):
        other_gram, other_proj = from_partner((gram_terms, projection), "leaf", bit_index)
        gram_terms = gram_terms + other_gram
        projection = projection + other_proj
    return (gram_terms, projection)


def local(coords, latent, labels, site_order, level_bases):
    scaled_bases, applied, vector = leaf_solve(coords, latent, labels, site_order[0], level_bases)
    level_count = level_bases.shape[0]
    total_bits = lax.axis_size("leaf").bit_length() - 1
    for level_idx in range(level_count):
        depth = total_bits - (level_count - 1 - level_idx)
        gram_terms, projection = node_terms(scaled_bases[level_idx], applied, vector)
        gram_terms, projection = node_sum_whole(gram_terms, projection, depth)
        coefficients, coeff_vector = core_solve(gram_terms, projection)
        applied, vector = apply_update(applied, vector, coefficients, coeff_vector)
    return vector


def solution(mesh):
    placed = (P(None, "leaf"), P("leaf"), P("leaf"), P("leaf", None), P(None, None, "leaf"))
    return jax.shard_map(local, mesh=mesh, in_specs=placed, out_specs=P("leaf"), check_vma=False)
```

profile of v0, /device:TPU:1, one launch (start us, length us, event | category | flops | bytes accessed | tf_op | source)
XLA Modules:
  0.0 872.7 jit_solution(1019008619427921671)
XLA Ops:
  17.3 11.7 %cholesky.136 = f32[128,128]{1,0:T(8,128)S(1)} custom-call(f32[128,128]{1,0:T(8,128)S(1)} %cholesky.531), custom_call_target="Cholesky" | custom-call | tf_op jit(solution)/shard_map/jit(cholesky)/cholesky | solution.py:36
  29.2 9.8 %custom-call.64 = f32[1,128,128]{1,2,0:T(8,128)S(1)} custom-call(f32[1,128,128]{2,1,0:T(8,128)S(1)} %get-tuple-element.122), custom_call_target="InvertDiagBlocksLowerTriangular" | custom-call | tf_op jit(solution)/shard_map/jit(cholesky)/cholesky | solution.py:36
  41.5 11.9 %cholesky.159 = f32[128,128]{1,0:T(8,128)S(1)} custom-call(f32[128,128]{1,0:T(8,128)S(1)} %cholesky.535), custom_call_target="Cholesky" | custom-call | tf_op jit(solution)/shard_map/jit(cholesky)/cholesky | solution.py:36
  53.5 9.8 %custom-call.65 = f32[1,128,128]{1,2,0:T(8,128)S(1)} custom-call(f32[1,128,128]{2,1,0:T(8,128)S(1)} %get-tuple-element.119), custom_call_target="InvertDiagBlocksLowerTriangular" | custom-call | tf_op jit(solution)/shard_map/jit(cholesky)/cholesky | solution.py:36
  64.8 11.7 %cholesky.294 = f32[128,128]{1,0:T(8,128)S(1)} custom-call(f32[128,128]{1,0:T(8,128)S(1)} %cholesky.540), custom_call_target="Cholesky" | custom-call | tf_op jit(solution)/shard_map/jit(cholesky)/cholesky | solution.py:36
  76.6 9.8 %custom-call.79 = f32[1,128,128]{1,2,0:T(8,128)S(1)} custom-call(f32[1,128,128]{2,1,0:T(8,128)S(1)} %get-tuple-element.116), custom_call_target="InvertDiagBlocksLowerTriangular" | custom-call | tf_op jit(solution)/shard_map/jit(cholesky)/cholesky/custom-call.18 | solution.py:36
  87.9 12.1 %cholesky.307 = f32[128,128]{1,0:T(8,128)S(1)} custom-call(f32[128,128]{1,0:T(8,128)S(1)} %convolution_subtract_fusion.17), custom_call_target="Cholesky" | custom-call | tf_op jit(solution)/shard_map/jit(cholesky)/cholesky | solution.py:36
  105.8 14.0 %while.5 = (s32[]{:T(128)}, f32[512,512]{1,0:T(8,128)}, s32[4,2]{0,1:T(2,128)S(1)}, f32[4,128,128]{2,1,0:T(8,128)}, s32[]{:T(128)}) while((s32[]{:T(128)}, f32[512,512]{1,0:T(8,128)}, s32[4,2]{0,1:T(2,128)S(1)}, f32[4,128,128]{2,1,0:T(8,128)}, s32[]{:T(128)}) %tuple.97), condition=%wide.while_cond, body=%wide.while_body.sunk | while | flops 2 | bytes 132205 | solution.py:39
  119.8 40.2 %custom-call.66 = f32[4,128,128]{1,2,0:T(8,128)S(1)} custom-call(f32[4,128,128]{2,1,0:T(8,128)} %get-tuple-element.14), custom_call_target="InvertDiagBlocksLowerTriangular" | custom-call | tf_op jit(solution)/shard_map/jit(_cho_solve)/triangular_solve | solution.py:39
  183.8 24.3 %collective-permute-done.1 = f32[4,256,256]{1,2,0:T(8,128)S(1)} collective-permute-done((f32[4,256,256]{1,2,0:T(8,128)S(1)}, f32[4,256,256]{1,2,0:T(8,128)S(1)}, u32[]{:S(2)}, u32[]{:S(2)}) %collective-permute-start.1) | collective-permute-done | bytes 1048608 | tf_op jit(solution)/shard_map/ppermute | solution.py:17
  209.5 23.8 %collective-permute-done.2 = f32[4,256,256]{1,2,0:T(8,128)S(1)} collective-permute-done((f32[4,256,256]{1,2,0:T(8,128)S(1)}, f32[4,256,256]{1,2,0:T(8,128)S(1)}, u32[]{:S(2)}, u32[]{:S(2)}) %collective-permute-start.2) | collective-permute-done | bytes 1048608 | tf_op jit(solution)/shard_map/ppermute | solution.py:17
  233.6 22.6 %collective-permute-done.3 = f32[4,256,256]{1,2,0:T(8,128)S(1)} collective-permute-done((f32[4,256,256]{1,2,0:T(8,128)S(1)}, f32[4,256,256]{1,2,0:T(8,128)S(1)}, u32[]{:S(2)}, u32[]{:S(2)}) %collective-permute-start.3) | collective-permute-done | bytes 1048608 | tf_op jit(solution)/shard_map/ppermute | solution.py:17
  269.4 8.8 %collective-permute-done.8 = f32[256]{0:T(256)S(1)} collective-permute-done((f32[256]{0:T(256)S(1)}, f32[256]{0:T(256)S(1)}, u32[]{:S(2)}, u32[]{:S(2)}) %collective-permute-start.8) | collective-permute-done | bytes 1056 | tf_op jit(solution)/shard_map/ppermute | solution.py:17
  288.3 11.7 %cholesky.427 = f32[128,128]{1,0:T(8,128)S(1)} custom-call(f32[128,128]{1,0:T(8,128)S(1)} %cholesky.544), custom_call_target="Cholesky" | custom-call | tf_op jit(solution)/shard_map/jit(cholesky)/cholesky | solution.py:54
  300.0 9.8 %custom-call.80 = f32[1,128,128]{1,2,0:T(8,128)S(1)} custom-call(f32[1,128,128]{2,1,0:T(8,128)S(1)} %get-tuple-element.112), custom_call_target="InvertDiagBlocksLowerTriangular" | custom-call | tf_op jit(solution)/shard_map/jit(cholesky)/cholesky/custom-call.18 | solution.py:54
  312.0 11.7 %cholesky.437 = f32[128,128]{1,0:T(8,128)S(1)} custom-call(f32[128,128]{1,0:T(8,128)S(1)} %convolution_subtract_fusion.16), custom_call_target="Cholesky" | custom-call | tf_op jit(solution)/shard_map/jit(cholesky)/cholesky | solution.py:54
  330.9 19.7 %custom-call.67 = f32[2,128,128]{1,2,0:T(8,128)S(1)} custom-call(f32[2,128,128]{2,1,0:T(8,128)S(1)} %get-tuple-element.22), custom_call_target="InvertDiagBlocksLowerTriangular" | custom-call | tf_op jit(solution)/shard_map/jit(_cho_solve)/triangular_solve | solution.py:62
  365.1 17.8 %collective-permute-done.11 = f32[3,256,256]{1,2,0:T(8,128)S(1)} collective-permute-done((f32[3,256,256]{1,2,0:T(8,128)S(1)}, f32[3,256,256]{1,2,0:T(8,128)S(1)}, u32[]{:S(2)}, u32[]{:S(2)}) %collective-permute-start.11) | collective-permute-done | bytes 786464 | tf_op jit(solution)/shard_map/ppermute | solution.py:17
  385.7 16.8 %collective-permute-done.12 = f32[3,256,256]{1,2,0:T(8,128)S(1)} collective-permute-done((f32[3,256,256]{1,2,0:T(8,128)S(1)}, f32[3,256,256]{1,2,0:T(8,128)S(1)}, u32[]{:S(2)}, u32[]{:S(2)}) %collective-permute-start.12) | collective-permute-done | bytes 786464 | tf_op jit(solution)/shard_map/ppermute | solution.py:17
  403.5 16.2 %collective-permute-done.13 = f32[3,256,256]{1,2,0:T(8,128)S(1)} collective-permute-done((f32[3,256,256]{1,2,0:T(8,128)S(1)}, f32[3,256,256]{1,2,0:T(8,128)S(1)}, u32[]{:S(2)}, u32[]{:S(2)}) %collective-permute-start.13) | collective-permute-done | bytes 786464 | tf_op jit(solution)/shard_map/ppermute | solution.py:17
  422.0 15.5 %collective-permute-done.14 = f32[3,256,256]{1,2,0:T(8,128)S(1)} collective-permute-done((f32[3,256,256]{1,2,0:T(8,128)S(1)}, f32[3,256,256]{1,2,0:T(8,128)S(1)}, u32[]{:S(2)}, u32[]{:S(2)}) %collective-permute-start.14) | collective-permute-done | bytes 786464 | tf_op jit(solution)/shard_map/ppermute | solution.py:17
  467.2 11.7 %cholesky.454 = f32[128,128]{1,0:T(8,128)S(1)} custom-call(f32[128,128]{1,0:T(8,128)S(1)} %cholesky.547), custom_call_target="Cholesky" | custom-call | tf_op jit(solution)/shard_map/jit(cholesky)/cholesky | solution.py:54
  479.0 9.8 %custom-call.81 = f32[1,128,128]{1,2,0:T(8,128)S(1)} custom-call(f32[1,128,128]{2,1,0:T(8,128)S(1)} %get-tuple-element.108), custom_call_target="InvertDiagBlocksLowerTriangular" | custom-call | tf_op jit(solution)/shard_map/jit(cholesky)/cholesky/custom-call.18 | solution.py:54
  491.0 11.7 %cholesky.464 = f32[128,128]{1,0:T(8,128)S(1)} custom-call(f32[128,128]{1,0:T(8,128)S(1)} %convolution_subtract_fusion.15), custom_call_target="Cholesky" | custom-call | tf_op jit(solution)/shard_map/jit(cholesky)/cholesky | solution.py:54
  509.8 19.7 %custom-call.68 = f32[2,128,128]{1,2,0:T(8,128)S(1)} custom-call(f32[2,128,128]{2,1,0:T(8,128)S(1)} %get-tuple-element.30), custom_call_target="InvertDiagBlocksLowerTriangular" | custom-call | tf_op jit(solution)/shard_map/jit(_cho_solve)/triangular_solve | solution.py:62
  535.1 5.1 collective-permute-start.22
  543.2 11.8 %collective-permute-done.23 = f32[2,256,256]{1,2,0:T(8,128)S(1)} collective-permute-done((f32[2,256,256]{1,2,0:T(8,128)S(1)}, f32[2,256,256]{1,2,0:T(8,128)S(1)}, u32[]{:S(2)}, u32[]{:S(2)}) %collective-permute-start.23) | collective-permute-done | bytes 524320 | tf_op jit(solution)/shard_map/ppermute | solution.py:17
  558.1 10.8 %collective-permute-done.24 = f32[2,256,256]{1,2,0:T(8,128)S(1)} collective-permute-done((f32[2,256,256]{1,2,0:T(8,128)S(1)}, f32[2,256,256]{1,2,0:T(8,128)S(1)}, u32[]{:S(2)}, u32[]{:S(2)}) %collective-permute-start.24) | collective-permute-done | bytes 524320 | tf_op jit(solution)/shard_map/ppermute | solution.py:17
  570.3 10.2 %collective-permute-done.25 = f32[2,256,256]{1,2,0:T(8,128)S(1)} collective-permute-done((f32[2,256,256]{1,2,0:T(8,128)S(1)}, f32[2,256,256]{1,2,0:T(8,128)S(1)}, u32[]{:S(2)}, u32[]{:S(2)}) %collective-permute-start.25) | collective-permute-done | bytes 524320 | tf_op jit(solution)/shard_map/ppermute | solution.py:17
  582.4 10.3 %collective-permute-done.26 = f32[2,256,256]{1,2,0:T(8,128)S(1)} collective-permute-done((f32[2,256,256]{1,2,0:T(8,128)S(1)}, f32[2,256,256]{1,2,0:T(8,128)S(1)}, u32[]{:S(2)}, u32[]{:S(2)}) %collective-permute-start.26) | collective-permute-done | bytes 524320 | tf_op jit(solution)/shard_map/ppermute | solution.py:17
  593.1 9.5 %collective-permute-done.27 = f32[2,256,256]{1,2,0:T(8,128)S(1)} collective-permute-done((f32[2,256,256]{1,2,0:T(8,128)S(1)}, f32[2,256,256]{1,2,0:T(8,128)S(1)}, u32[]{:S(2)}, u32[]{:S(2)}) %collective-permute-start.27) | collective-permute-done | bytes 524320 | tf_op jit(solution)/shard_map/ppermute | solution.py:17
  607.7 6.3 collective-permute-start.29
  640.5 11.7 %cholesky.481 = f32[128,128]{1,0:T(8,128)S(1)} custom-call(f32[128,128]{1,0:T(8,128)S(1)} %cholesky.550), custom_call_target="Cholesky" | custom-call | tf_op jit(solution)/shard_map/jit(cholesky)/cholesky | solution.py:54
  653.0 9.8 %custom-call.82 = f32[1,128,128]{1,2,0:T(8,128)S(1)} custom-call(f32[1,128,128]{2,1,0:T(8,128)S(1)} %get-tuple-element.104), custom_call_target="InvertDiagBlocksLowerTriangular" | custom-call | tf_op jit(solution)/shard_map/jit(cholesky)/cholesky/custom-call.18 | solution.py:54
  665.6 11.7 %cholesky.491 = f32[128,128]{1,0:T(8,128)S(1)} custom-call(f32[128,128]{1,0:T(8,128)S(1)} %convolution_subtract_fusion.14), custom_call_target="Cholesky" | custom-call | tf_op jit(solution)/shard_map/jit(cholesky)/cholesky | solution.py:54
  682.2 5.8 while.8
  688.6 20.5 %custom-call.69 = f32[2,128,128]{1,2,0:T(8,128)S(1)} custom-call(f32[2,128,128]{2,1,0:T(8,128)} %copy-done.18), custom_call_target="InvertDiagBlocksLowerTriangular" | custom-call | tf_op jit(solution)/shard_map/jit(_cho_solve)/triangular_solve | solution.py:62
  714.4 6.5 collective-permute-start.36
  723.5 6.2 collective-permute-done.37
  732.7 5.2 collective-permute-done.38
  745.7 5.0 collective-permute-done.40
  750.8 5.2 collective-permute-done.41
  756.2 8.8 %collective-permute-done.42 = f32[1,256,256]{1,2,0:T(8,128)S(1)} collective-permute-done((f32[1,256,256]{1,2,0:T(8,128)S(1)}, f32[1,256,256]{1,2,0:T(8,128)S(1)}, u32[]{:S(2)}, u32[]{:S(2)}) %collective-permute-start.42) | collective-permute-done | bytes 262176 | tf_op jit(solution)/shard_map/ppermute | solution.py:17
  769.0 13.9 %collective-permute-start.44 = (f32[256]{0:T(256)S(1)}, f32[256]{0:T(256)S(1)}, u32[]{:S(2)}, u32[]{:S(2)}) collective-permute-start(f32[256]{0:T(256)S(1)} %bitcast.410), channel_id=1, source_target_pairs={{0,1},{1,0},{2,3},{3,2},{4,5},{5,4},{6,7},{7,6},{8,9},{9,8},{10,11... | collective-permute-start | bytes 3080 | tf_op jit(solution)/shard_map/ppermute | solution.py:17
  809.6 11.7 %cholesky.508 = f32[128,128]{1,0:T(8,128)S(1)} custom-call(f32[128,128]{1,0:T(8,128)S(1)} %cholesky.553), custom_call_target="Cholesky" | custom-call | tf_op jit(solution)/shard_map/jit(cholesky)/cholesky | solution.py:54
  821.3 9.8 %custom-call.83 = f32[1,128,128]{1,2,0:T(8,128)S(1)} custom-call(f32[1,128,128]{2,1,0:T(8,128)S(1)} %get-tuple-element.100), custom_call_target="InvertDiagBlocksLowerTriangular" | custom-call | tf_op jit(solution)/shard_map/jit(cholesky)/cholesky/custom-call.18 | solution.py:54
  831.6 11.7 %cholesky.518 = f32[128,128]{1,0:T(8,128)S(1)} custom-call(f32[128,128]{1,0:T(8,128)S(1)} %convolution_subtract_fusion.13), custom_call_target="Cholesky" | custom-call | tf_op jit(solution)/shard_map/jit(cholesky)/cholesky | solution.py:54
  850.5 19.7 %custom-call.70 = f32[2,128,128]{1,2,0:T(8,128)S(1)} custom-call(f32[2,128,128]{2,1,0:T(8,128)S(1)} %get-tuple-element.46), custom_call_target="InvertDiagBlocksLowerTriangular" | custom-call | tf_op jit(solution)/shard_map/jit(_cho_solve)/triangular_solve | solution.py:62
  (367 shorter events, 285.1 us)
Async XLA Ops:
  177.9 5.6 collective-permute-start
  183.7 24.4 %collective-permute-start.1 = (f32[4,256,256]{1,2,0:T(8,128)S(1)}, f32[4,256,256]{1,2,0:T(8,128)S(1)}, u32[]{:S(2)}, u32[]{:S(2)}) collective-permute-start(f32[4,256,256]{1,2,0:T(8,128)S(1)} %add.359), channel_id=1, source_target_pairs={{0,2},{1,3},{2,0},{3,1},{4,6},{5,7},{6,4},{7,5},{8,10},{9,11},{10,... | collective-permute-start | bytes 3145736 | tf_op jit(solution)/shard_map/ppermute | solution.py:17
  208.2 25.1 %collective-permute-start.2 = (f32[4,256,256]{1,2,0:T(8,128)S(1)}, f32[4,256,256]{1,2,0:T(8,128)S(1)}, u32[]{:S(2)}, u32[]{:S(2)}) collective-permute-start(f32[4,256,256]{1,2,0:T(8,128)S(1)} %add.360), channel_id=1, source_target_pairs={{0,4},{1,5},{2,6},{3,7},{4,0},{5,1},{6,2},{7,3},{8,12},{9,13},{10,... | collective-permute-start | bytes 3145736 | tf_op jit(solution)/shard_map/ppermute | solution.py:17
  233.5 22.7 %collective-permute-start.3 = (f32[4,256,256]{1,2,0:T(8,128)S(1)}, f32[4,256,256]{1,2,0:T(8,128)S(1)}, u32[]{:S(2)}, u32[]{:S(2)}) collective-permute-start(f32[4,256,256]{1,2,0:T(8,128)S(1)} %add.361), channel_id=1, source_target_pairs={{0,8},{1,9},{2,10},{3,11},{4,12},{5,13},{6,14},{7,15},{8,0},{9,1},... | collective-permute-start | bytes 3145736 | tf_op jit(solution)/shard_map/ppermute | solution.py:17
  256.3 27.7 %collective-permute-start.4 = (f32[4,256,256]{1,2,0:T(8,128)S(1)}, f32[4,256,256]{1,2,0:T(8,128)}, u32[]{:S(2)}, u32[]{:S(2)}) collective-permute-start(f32[4,256,256]{1,2,0:T(8,128)S(1)} %add.362), channel_id=1, source_target_pairs={{0,16},{1,17},{2,18},{3,19},{4,20},{5,21},{6,22},{7,23},{8,24},{9,... | collective-permute-start | bytes 3145736 | tf_op jit(solution)/shard_map/ppermute | solution.py:17
  258.0 4.1 collective-permute-start.5
  262.0 2.8 collective-permute-start.6
  264.9 4.3 collective-permute-start.7
  269.2 9.0 %collective-permute-start.8 = (f32[256]{0:T(256)S(1)}, f32[256]{0:T(256)S(1)}, u32[]{:S(2)}, u32[]{:S(2)}) collective-permute-start(f32[256]{0:T(256)S(1)} %add.367), channel_id=1, source_target_pairs={{0,8},{1,9},{2,10},{3,11},{4,12},{5,13},{6,14},{7,15},{8,0},{9,1},... | collective-permute-start | bytes 3080 | tf_op jit(solution)/shard_map/ppermute | solution.py:17
  278.2 5.8 collective-permute-start.9
  358.3 5.7 collective-permute-start.10
  364.1 18.8 %collective-permute-start.11 = (f32[3,256,256]{1,2,0:T(8,128)S(1)}, f32[3,256,256]{1,2,0:T(8,128)S(1)}, u32[]{:S(2)}, u32[]{:S(2)}) collective-permute-start(f32[3,256,256]{1,2,0:T(8,128)S(1)} %add.370), channel_id=1, source_target_pairs={{0,2},{1,3},{2,0},{3,1},{4,6},{5,7},{6,4},{7,5},{8,10},{9,11},{10,... | collective-permute-start | bytes 2359304 | tf_op jit(solution)/shard_map/ppermute | solution.py:17
  383.0 19.5 %collective-permute-start.12 = (f32[3,256,256]{1,2,0:T(8,128)S(1)}, f32[3,256,256]{1,2,0:T(8,128)S(1)}, u32[]{:S(2)}, u32[]{:S(2)}) collective-permute-start(f32[3,256,256]{1,2,0:T(8,128)S(1)} %add.371), channel_id=1, source_target_pairs={{0,4},{1,5},{2,6},{3,7},{4,0},{5,1},{6,2},{7,3},{8,12},{9,13},{10,... | collective-permute-start | bytes 2359304 | tf_op jit(solution)/shard_map/ppermute | solution.py:17
  402.6 17.1 %collective-permute-start.13 = (f32[3,256,256]{1,2,0:T(8,128)S(1)}, f32[3,256,256]{1,2,0:T(8,128)S(1)}, u32[]{:S(2)}, u32[]{:S(2)}) collective-permute-start(f32[3,256,256]{1,2,0:T(8,128)S(1)} %add.372), channel_id=1, source_target_pairs={{0,8},{1,9},{2,10},{3,11},{4,12},{5,13},{6,14},{7,15},{8,0},{9,1},... | collective-permute-start | bytes 2359304 | tf_op jit(solution)/shard_map/ppermute | solution.py:17
  419.8 17.8 %collective-permute-start.14 = (f32[3,256,256]{1,2,0:T(8,128)S(1)}, f32[3,256,256]{1,2,0:T(8,128)S(1)}, u32[]{:S(2)}, u32[]{:S(2)}) collective-permute-start(f32[3,256,256]{1,2,0:T(8,128)S(1)} %add.373), channel_id=1, source_target_pairs={{0,16},{1,17},{2,18},{3,19},{4,20},{5,21},{6,22},{7,23},{8,24},{9,... | collective-permute-start | bytes 2359304 | tf_op jit(solution)/shard_map/ppermute | solution.py:17
  437.7 23.8 %collective-permute-start.15 = (f32[3,256,256]{1,2,0:T(8,128)S(1)}, f32[3,256,256]{1,2,0:T(8,128)}, u32[]{:S(2)}, u32[]{:S(2)}) collective-permute-start(f32[3,256,256]{1,2,0:T(8,128)S(1)} %add.374), channel_id=1, source_target_pairs={{0,32},{1,33},{2,34},{3,35},{4,36},{5,37},{6,38},{7,39},{8,40},{9,... | collective-permute-start | bytes 2359304 | tf_op jit(solution)/shard_map/ppermute | solution.py:17
  439.9 4.9 collective-permute-start.16
  444.8 2.8 collective-permute-start.17
  447.6 3.9 collective-permute-start.18
  451.6 2.8 collective-permute-start.19
  454.4 3.9 collective-permute-start.20
  458.3 3.1 collective-permute-start.21
  535.1 6.6 collective-permute-start.22
  541.8 13.2 %collective-permute-start.23 = (f32[2,256,256]{1,2,0:T(8,128)S(1)}, f32[2,256,256]{1,2,0:T(8,128)S(1)}, u32[]{:S(2)}, u32[]{:S(2)}) collective-permute-start(f32[2,256,256]{1,2,0:T(8,128)S(1)} %add.383), channel_id=1, source_target_pairs={{0,2},{1,3},{2,0},{3,1},{4,6},{5,7},{6,4},{7,5},{8,10},{9,11},{10,... | collective-permute-start | bytes 1572872 | tf_op jit(solution)/shard_map/ppermute | solution.py:17
  555.1 13.8 %collective-permute-start.24 = (f32[2,256,256]{1,2,0:T(8,128)S(1)}, f32[2,256,256]{1,2,0:T(8,128)S(1)}, u32[]{:S(2)}, u32[]{:S(2)}) collective-permute-start(f32[2,256,256]{1,2,0:T(8,128)S(1)} %add.384), channel_id=1, source_target_pairs={{0,4},{1,5},{2,6},{3,7},{4,0},{5,1},{6,2},{7,3},{8,12},{9,13},{10,... | collective-permute-start | bytes 1572872 | tf_op jit(solution)/shard_map/ppermute | solution.py:17
  569.0 11.5 %collective-permute-start.25 = (f32[2,256,256]{1,2,0:T(8,128)S(1)}, f32[2,256,256]{1,2,0:T(8,128)S(1)}, u32[]{:S(2)}, u32[]{:S(2)}) collective-permute-start(f32[2,256,256]{1,2,0:T(8,128)S(1)} %add.385), channel_id=1, source_target_pairs={{0,8},{1,9},{2,10},{3,11},{4,12},{5,13},{6,14},{7,15},{8,0},{9,1},... | collective-permute-start | bytes 1572872 | tf_op jit(solution)/shard_map/ppermute | solution.py:17
  580.6 12.1 %collective-permute-start.26 = (f32[2,256,256]{1,2,0:T(8,128)S(1)}, f32[2,256,256]{1,2,0:T(8,128)S(1)}, u32[]{:S(2)}, u32[]{:S(2)}) collective-permute-start(f32[2,256,256]{1,2,0:T(8,128)S(1)} %add.386), channel_id=1, source_target_pairs={{0,16},{1,17},{2,18},{3,19},{4,20},{5,21},{6,22},{7,23},{8,24},{9,... | collective-permute-start | bytes 1572872 | tf_op jit(solution)/shard_map/ppermute | solution.py:17
  592.8 9.8 %collective-permute-start.27 = (f32[2,256,256]{1,2,0:T(8,128)S(1)}, f32[2,256,256]{1,2,0:T(8,128)S(1)}, u32[]{:S(2)}, u32[]{:S(2)}) collective-permute-start(f32[2,256,256]{1,2,0:T(8,128)S(1)} %add.387), channel_id=1, source_target_pairs={{0,32},{1,33},{2,34},{3,35},{4,36},{5,37},{6,38},{7,39},{8,40},{9,... | collective-permute-start | bytes 1572872 | tf_op jit(solution)/shard_map/ppermute | solution.py:17
  603.4 30.7 %collective-permute-start.28 = (f32[2,256,256]{1,2,0:T(8,128)}, f32[2,256,256]{1,2,0:T(8,128)}, u32[]{:S(2)}, u32[]{:S(2)}) collective-permute-start(f32[2,256,256]{1,2,0:T(8,128)} %add.388), channel_id=1, source_target_pairs={{0,64},{1,65},{2,66},{3,67},{4,68},{5,69},{6,70},{7,71},{8,72},{9,... | collective-permute-start | bytes 1572872 | tf_op jit(solution)/shard_map/ppermute | solution.py:17
  607.7 7.1 collective-permute-start.29
  617.3 3.9 collective-permute-start.31
  621.2 2.8 collective-permute-start.32
  624.0 3.9 collective-permute-start.33
  628.0 2.8 collective-permute-start.34
  630.8 3.3 collective-permute-start.35
  714.4 7.7 collective-permute-start.36
  722.1 7.6 collective-permute-start.37
  729.7 8.2 collective-permute-start.38
  737.9 5.9 collective-permute-start.39
  743.9 6.8 collective-permute-start.40
  750.7 5.3 collective-permute-start.41
  756.1 8.9 %collective-permute-start.42 = (f32[1,256,256]{1,2,0:T(8,128)S(1)}, f32[1,256,256]{1,2,0:T(8,128)S(1)}, u32[]{:S(2)}, u32[]{:S(2)}) collective-permute-start(f32[1,256,256]{1,2,0:T(8,128)S(1)} %add.403), channel_id=1, source_target_pairs={{0,64},{1,65},{2,66},{3,67},{4,68},{5,69},{6,70},{7,71},{8,72},{9,... | collective-permute-start | bytes 786440 | tf_op jit(solution)/shard_map/ppermute | solution.py:17
  765.0 44.3 %collective-permute-start.43 = (f32[1,256,256]{1,2,0:T(8,128)S(1)}, f32[1,256,256]{1,2,0:T(8,128)S(1)}, u32[]{:S(2)}, u32[]{:S(2)}) collective-permute-start(f32[1,256,256]{1,2,0:T(8,128)S(1)} %add.404), channel_id=1, source_target_pairs={{0,128},{1,129},{2,130},{3,131},{4,132},{5,133},{6,134},{7,135},{8... | collective-permute-start | bytes 786440 | tf_op jit(solution)/shard_map/ppermute | solution.py:17
  769.0 14.7 %collective-permute-start.44 = (f32[256]{0:T(256)S(1)}, f32[256]{0:T(256)S(1)}, u32[]{:S(2)}, u32[]{:S(2)}) collective-permute-start(f32[256]{0:T(256)S(1)} %bitcast.410), channel_id=1, source_target_pairs={{0,1},{1,0},{2,3},{3,2},{4,5},{5,4},{6,7},{7,6},{8,9},{9,8},{10,11... | collective-permute-start | bytes 3080 | tf_op jit(solution)/shard_map/ppermute | solution.py:17
  786.4 4.2 collective-permute-start.46
  793.1 3.9 collective-permute-start.48
  799.4 3.3 collective-permute-start.50
  802.8 6.5 collective-permute-start.51
  (25 other events, 276.7 us)
where the time goes:
time: 890 us; the launch traced here: 873 us
  other arithmetic  359 us (40%)
  waiting for transfers between devices  284 us (32%)
  starting transfers between devices  110 us (12%)
  local copies, waits for them, and re-layouts  54.8 us (6%)
  matrix products  53.6 us (6%)
  between operations  9.37 us (1%)
    ppermute x52, waiting for transfers between devices, from_partner(): return lax.ppermute(value, axis, pairs)  284 us
    another operation x28, other arithmetic, core_solve(): core_factor = jnp.linalg.cholesky(core_matrix)  139 us
    ppermute x52, starting transfers between devices, from_partner(): return lax.ppermute(value, axis, pairs)  110 us
    another operation x11, other arithmetic, core_solve(): solution = jax.scipy.linalg.cho_solve((core_factor, True), right_hand)  81.4 us
    another operation x14, other arithmetic, leaf_solve(): factor = jnp.linalg.cholesky(leaf_matrix)  79 us
    another operation x4, other arithmetic, leaf_solve(): solved = jax.scipy.linalg.cho_solve((factor, True), stacked)  41.5 us
    another operation x36, local copies, waits for them, and re-layouts  31.8 us
  transfers between devices with their start and end apart: 52, of which 47 were waited for; matrix products, arithmetic and copies ran while one was open for 1% of the time, Pallas kernels for 0%

commit v1 on v0

v1 whole, which is shorter than its diff:
```python
import functools
import math

import jax
import jax.numpy as jnp
from jax import lax
from jax.experimental import pallas as pl
from jax.experimental.pallas import tpu as pltpu
from jax.sharding import PartitionSpec as P

F32 = jnp.float32
BF16 = jnp.bfloat16
HIGHEST = lax.Precision.HIGHEST
LENGTH_SCALE = 0.25
VARIANCE = 16.0
ROOT_FIVE = math.sqrt(5.0)
M = 512
R = 256
LEVELS = 4
LANES = 128
PLANE = 32
NN = (((1,), (0,)), ((), ()))
NT = (((1,), (1,)), ((), ()))


def dot(a, b, dims=NN):
    return lax.dot_general(a, b, dims, preferred_element_type=F32)


def dot_f32(a, b, dims=NN):
    return lax.dot_general(a, b, dims, precision=HIGHEST, preferred_element_type=F32)


def split(x):
    hi = x.astype(BF16)
    return hi, (x - hi.astype(F32)).astype(BF16)


def split3(x):
    hi = x.astype(BF16)
    rest = x - hi.astype(F32)
    mid = rest.astype(BF16)
    return hi, mid, (rest - mid.astype(F32)).astype(BF16)


def dot3(a, b, dims=NN):
    return dot(a[0], b[0], dims) + (dot(a[0], b[1], dims) + dot(a[1], b[0], dims))


def eye(n):
    return jnp.where(
        lax.broadcasted_iota(jnp.int32, (n, n), 0) == lax.broadcasted_iota(jnp.int32, (n, n), 1), 1.0, 0.0
    ).astype(F32)


def newton_inverse(s, z_ref):
    n = s.shape[0]
    bound = jnp.max(jnp.sum(jnp.abs(s), axis=0, keepdims=True))
    alpha = 2.0 / (1.0 + bound)
    gap = (bound - 1.0) / (bound + 1.0)
    scale = 2.0 / (2.0 - gap * gap)
    z_ref[...] = (alpha * scale) * (2.0 * eye(n) - alpha * s)
    gap = gap * gap / (2.0 - gap * gap)
    parts = split(s)

    def body(gap):
        z = z_ref[...]
        zs = split(z)
        residual = eye(n) - dot3(parts, zs)
        scale = 2.0 / (2.0 - gap * gap)
        z_ref[...] = scale * (z + dot3(zs, split(residual)))
        return gap * gap / (2.0 - gap * gap)

    lax.while_loop(lambda gap: gap > 2e-3, body, gap)
    z = z_ref[...]
    residual = eye(n) - dot_f32(s, z)
    return z + dot3(split(z), split(residual))


def leaf_kernel(coord_ref, latent_ref, label_ref, order_ref, basis_ref, front_ref, inverse_ref, rows_ref,
                a_ref, z_ref, mh_ref, ml_ref):
    picked = lax.broadcasted_iota(jnp.int32, (M, M), 0) == order_ref[...]
    one_hot = jnp.where(picked, 1.0, 0.0).astype(BF16)
    hi, mid, lo = split3(latent_ref[...])
    row = lax.broadcasted_iota(jnp.int32, (16, M), 0)
    packed = jnp.where(row == 0, hi.astype(F32), 0.0)
    packed = jnp.where(row == 1, mid.astype(F32), packed)
    packed = jnp.where(row == 2, lo.astype(F32), packed)
    packed = jnp.where(row == 3, label_ref[...].astype(F32), packed)
    got = dot(packed.astype(BF16), one_hot)
    tree_latent = (got[0:1] + got[1:2]) + got[2:3]
    tree_target = got[3:4]
    probability = 1.0 / (1.0 + jnp.exp(-tree_latent))
    weight = probability * (1.0 - probability)
    root_weight = jnp.sqrt(weight)
    right_side = root_weight * (weight * tree_latent + tree_target - probability)

    def column(value, i):
        return jnp.broadcast_to(value[:, i * LANES:(i + 1) * LANES], (LANES, LANES)).T

    axes = [coord_ref[k:k + 1, :] for k in range(3)]
    columns = []
    for i in range(4):
        cols = [column(axis, i) for axis in axes]
        weight_col = column(root_weight, i)
        columns.append(weight_col)
        for j in range(i, 4):
            span = slice(j * LANES, (j + 1) * LANES)
            total = None
            for axis, col in zip(axes, cols):
                difference = col - axis[:, span]
                total = difference * difference if total is None else total + difference * difference
            scaled = (ROOT_FIVE / LENGTH_SCALE) * jnp.sqrt(total)
            kernel = VARIANCE * (1.0 + scaled + scaled * scaled / 3.0) * jnp.exp(-scaled)
            block = weight_col * kernel * root_weight[:, span]
            if i == j:
                block = block + eye(LANES)
            a_ref[i * LANES:(i + 1) * LANES, span] = block
            if i != j:
                a_ref[span, i * LANES:(i + 1) * LANES] = block.T

    top, bottom = slice(0, R), slice(R, M)
    x = newton_inverse(a_ref[top, top], z_ref)
    u = dot_f32(x, a_ref[top, bottom])
    v = dot_f32(a_ref[bottom, top], x)
    schur = newton_inverse(a_ref[bottom, bottom] - dot_f32(v, a_ref[top, bottom]), z_ref)
    us = dot_f32(u, schur)
    inverse_ref[bottom, bottom] = schur
    inverse_ref[top, bottom] = -us
    inverse_ref[bottom, top] = -dot_f32(schur, v)
    inverse_ref[top, top] = x + dot_f32(us, v)

    for i in range(4):
        for j in range(4):
            rows, span = slice(i * LANES, (i + 1) * LANES), slice(j * LANES, (j + 1) * LANES)
            hi, lo = split(columns[i] * inverse_ref[rows, span] * root_weight[:, span])
            mh_ref[rows, span] = hi
            ml_ref[rows, span] = lo
    solved = dot_f32(jnp.broadcast_to(right_side, (8, M)), inverse_ref[...])[0:1]
    weighted = split3(root_weight * solved)
    lane = lax.broadcasted_iota(jnp.int32, (LANES, M), 0)
    tile = jnp.zeros((R, LANES), F32)
    offset = 0
    for level in range(LEVELS):
        basis = basis_ref[level]
        part = split(dot(basis, mh_ref[...]) + dot(basis, ml_ref[...]))
        for other in range(level, LEVELS):
            front_ref[:, offset:offset + R] = dot(part[0], basis_ref[other], NT) + dot(part[1], basis_ref[other], NT)
            offset += R
        if level == 0:
            offset += LANES
        for piece in weighted:
            placed = jnp.where(lane == level, piece.astype(F32), 0.0).astype(BF16)
            tile = tile + dot(basis, placed, NT)
    front_ref[:, LEVELS * R:LEVELS * R + LANES] = tile
    row = lax.broadcasted_iota(jnp.int32, (8, M), 0)
    rows_ref[...] = jnp.where(row == 0, root_weight, right_side)


def vmem(n):
    return [pl.BlockSpec(memory_space=pltpu.VMEM)] * n


FRONT = LEVELS * R + LANES + 6 * R
PARAMS = pltpu.CompilerParams(vmem_limit_bytes=60 * 1024 * 1024)


def leaf_call(coords, latent, labels, order, bases):
    return pl.pallas_call(
        leaf_kernel,
        out_shape=(
            jax.ShapeDtypeStruct((R, FRONT), F32),
            jax.ShapeDtypeStruct((M, M), F32),
            jax.ShapeDtypeStruct((8, M), F32),
        ),
        in_specs=vmem(5),
        out_specs=tuple(vmem(3)),
        scratch_shapes=[
            pltpu.VMEM((M, M), F32), pltpu.VMEM((R, R), F32), pltpu.VMEM((M, M), BF16), pltpu.VMEM((M, M), BF16)
        ],
        compiler_params=PARAMS,
        name="leaf",
    )(coords, latent, labels, order, bases)


def eliminate(left, gathered_ref, z_ref):
    inverse = newton_inverse(gathered_ref[:, 0:R] + eye(R), z_ref)
    return dot3(split(inverse), split(gathered_ref[:, R:left * R + LANES]))


def level_kernel(left, gathered_ref, own_ref, next_ref, h_ref, z_ref):
    h = eliminate(left, gathered_ref, z_ref)
    h_ref[...] = h
    width = (left - 1) * R
    h_parts = split(h)
    mine = lax.rem(lax.axis_index("leaf"), PLANE) * 8
    wanted = lax.broadcasted_iota(jnp.int32, (8, R), 1) == lax.broadcasted_iota(jnp.int32, (8, R), 0) + mine
    one_hot = jnp.where(wanted, 1.0, 0.0).astype(BF16)
    lane = lax.broadcasted_iota(jnp.int32, (8, LANES), 1)
    tile = own_ref[:, left * R:left * R + LANES]
    source, target = left * R + LANES, 0
    for k in range(1, left):
        block = split3(gathered_ref[:, k * R:(k + 1) * R])
        rows = dot(one_hot, block[0], NT) + dot(one_hot, block[1], NT) + dot(one_hot, block[2], NT)
        drop = dot3(split(rows), h_parts)
        span = (left - k) * R
        next_ref[:, target:target + span] = own_ref[:, source:source + span] - drop[:, (k - 1) * R:width]
        source, target = source + span, target + span
        if k == 1:
            target += LANES
        at = LEVELS - left
        tile = tile - jnp.where(lane == at + k, drop[:, width + at:width + at + 1], 0.0)
    next_ref[:, width:width + LANES] = tile


def own_width(left):
    return LANES + R * (left * (left + 1) // 2)


def level_call(left, gathered, own):
    return pl.pallas_call(
        functools.partial(level_kernel, left),
        out_shape=(
            jax.ShapeDtypeStruct((8, own_width(left - 1)), F32),
            jax.ShapeDtypeStruct((R, (left - 1) * R + LANES), F32),
        ),
        in_specs=vmem(2),
        out_specs=tuple(vmem(2)),
        scratch_shapes=[pltpu.VMEM((R, R), F32)],
        compiler_params=PARAMS,
        name=f"level{LEVELS - left + 1}",
    )(gathered, own)


def last_kernel(gathered_ref, h1_ref, h2_ref, h3_ref, inverse_ref, rows_ref, basis_ref, out_ref, z_ref):
    h4 = eliminate(1, gathered_ref, z_ref)
    total = jnp.zeros((16, M), F32)
    later = []
    for level in reversed(range(LEVELS)):
        rest = LEVELS - 1 - level
        h_ref = (h1_ref, h2_ref, h3_ref, None)[level]
        tile = h4 if h_ref is None else h_ref[:, rest * R:rest * R + LANES]
        z = jnp.broadcast_to(tile.T[level:level + 1, :], (8, R))
        for k, done in enumerate(later):
            z = z - dot_f32(done, h_ref[:, k * R:(k + 1) * R], NT)
        later.insert(0, z)
        hi, mid, lo = split3(z[0:1])
        row = lax.broadcasted_iota(jnp.int32, (16, R), 0)
        packed = jnp.where(row == 0, hi.astype(F32), jnp.where(row == 1, mid.astype(F32), jnp.where(row == 2, lo.astype(F32), 0.0)))
        total = total + dot(packed.astype(BF16), basis_ref[level])
    spread = (total[0:1] + total[1:2]) + total[2:3]
    right = rows_ref[1:2] - rows_ref[0:1] * spread
    out_ref[...] = dot_f32(jnp.broadcast_to(right, (8, M)), inverse_ref[...])


def last_call(gathered, h1, h2, h3, inverse, rows, bases):
    return pl.pallas_call(
        last_kernel,
        out_shape=jax.ShapeDtypeStruct((8, M), F32),
        in_specs=vmem(7),
        out_specs=vmem(1)[0],
        scratch_shapes=[pltpu.VMEM((R, R), F32)],
        compiler_params=PARAMS,
        name="last",
    )(gathered, h1, h2, h3, inverse, rows, bases)


def planes(count):
    return [[p * PLANE + d for d in range(PLANE)] for p in range(count)]


def local(coords, latent, labels, site_order, level_bases):
    count = lax.axis_size("leaf")
    groups = planes(count // PLANE)
    front, inverse, rows = leaf_call(
        coords, latent.reshape(1, M), labels.reshape(1, M), site_order, level_bases
    )
    own = lax.psum_scatter(front, "leaf", axis_index_groups=groups, scatter_dimension=0, tiled=True)
    h = []
    for level in range(LEVELS):
        left = LEVELS - level
        if level > 0:
            bit = PLANE << (level - 1)
            own = own + lax.ppermute(own, "leaf", [(d, d ^ bit) for d in range(count)])
        gathered = lax.all_gather(
            own[:, :left * R + LANES], "leaf", axis_index_groups=groups, axis=0, tiled=True
        )
        if left > 1:
            own, part = level_call(left, gathered, own)
            h.append(part)
    return last_call(gathered, *h, inverse, rows, level_bases)[0]


def solution(mesh):
    placed = (P(None, "leaf"), P("leaf"), P("leaf"), P("leaf", None), P(None, None, "leaf"))
    return jax.shard_map(local, mesh=mesh, in_specs=placed, out_specs=P("leaf"), check_vma=False)
```

time: 890 us -> 337 us (0.38); the launches traced: 873 us -> 337 us
  other arithmetic: 359 us -> 2.28 us
  waiting for transfers between devices: 284 us -> 174 us
  starting transfers between devices: 110 us -> 9.35 us
  blocking collectives: 0 us -> 81.2 us
  matrix products: 53.6 us -> 0 us
  Pallas kernels: 0 us -> 51.3 us
  local copies, waits for them, and re-layouts: 54.8 us -> 4.81 us
    another operation x57 -> x0, other arithmetic: 341 us -> none  [the longest x28 139 us: core_solve(): core_factor = jnp.linalg.cholesky(core_matrix)]
    ppermute x52 -> x3, waiting for transfers between devices: 284 us -> 4.78 us  [local(): own = own + lax.ppermute(own, 'leaf', [(d, d ^ bit) for d in range(count)])]
    unnamed x0 -> x3, waiting for transfers between devices: none -> 122 us
    ppermute x52 -> x3, starting transfers between devices: 110 us -> 9.31 us  [local(): own = own + lax.ppermute(own, 'leaf', [(d, d ^ bit) for d in range(count)])]
    all_gather x0 -> x3, blocking collectives: none -> 81.2 us  [local(): lax.all_gather(own[:, :left * R + LANES], 'leaf', axis_index_groups=group...]
    pallas_call x0 -> x5, Pallas kernels: none -> 51.3 us  [the longest x3 22.7 us: level_call(): pl.pallas_call(functools.partial(level_kernel, left), out_shape=(jax.Shap...]
    all_gather x0 -> x1, waiting for transfers between devices: none -> 47.7 us  [local(): lax.all_gather(own[:, :left * R + LANES], 'leaf', axis_index_groups=group...]
    another operation x52 -> x0, matrix products: 42 us -> none  [the longest x14 15.8 us: leaf_solve(): solved = jax.scipy.linalg.cho_solve((factor, True), stacked)]
  transfers between devices with their start and end apart: 52 -> 5, of which waited for: 47 -> 5; matrix products, arithmetic and copies ran while one was open for 1% -> 1% of each run, Pallas kernels for 0% -> 0%
where the time goes in v1:
time: 337 us
  waiting for transfers between devices  174 us (52%)
  blocking collectives  81.2 us (24%)
  Pallas kernels  51.3 us (15%)
  between operations  14.1 us (4%)
  starting transfers between devices  9.35 us (3%)
  local copies, waits for them, and re-layouts  4.81 us (1%)
    unnamed x3, waiting for transfers between devices  122 us
    all_gather x3, blocking collectives, local(): lax.all_gather(own[:, :left * R + LANES], 'leaf', axis_index_groups=group...  81.2 us
    all_gather x1, waiting for transfers between devices, local(): lax.all_gather(own[:, :left * R + LANES], 'leaf', axis_index_groups=group...  47.7 us
    pallas_call x3, Pallas kernels, level_call(): pl.pallas_call(functools.partial(level_kernel, left), out_shape=(jax.Shap...  22.7 us
    pallas_call x1, Pallas kernels, leaf_call(): pl.pallas_call(leaf_kernel, out_shape=(jax.ShapeDtypeStruct((R, FRONT), F...  17.3 us
    pallas_call x1, Pallas kernels, last_call(): pl.pallas_call(last_kernel, out_shape=jax.ShapeDtypeStruct((8, M), F32),...  11.3 us
    ppermute x3, starting transfers between devices, local(): own = own + lax.ppermute(own, 'leaf', [(d, d ^ bit) for d in range(count)])  9.31 us
  transfers between devices with their start and end apart: 5, of which 5 were waited for; matrix products, arithmetic and copies ran while one was open for 1% of the time, Pallas kernels for 0%

profile of v1, /device:TPU:1, one launch (start us, length us, event | category | flops | bytes accessed | tf_op | source)
XLA Modules:
  0.0 337.1 jit_solution(4631519662660226606)
XLA Ops:
  6.5 0.0 copy-start.2
  6.5 0.0 all-reduce.3.cloned.1.call-start
  6.5 17.3 %leaf.1 = (f32[256,2688]{1,0:T(8,128)}, f32[512,512]{1,0:T(8,128)}, f32[8,512]{1,0:T(8,128)}) custom-call(f32[3,512]{1,0:T(4,128)} %coord_ref.1, f32[1,512]{1,0:T(1,128)} %bitcast.4, s32[1,512]{1,0:T(1,128)} %bitcast.5, s32[1,512]{1,0:T(1,128)} %order_ref.1, bf16[4,256,512]{2,1,0:T(8,128)(2,1)} %basis_ref.3), custom_call_target="tpu_custom_call" | custom-call | tf_op jit(solution)/shard_map/leaf/pallas_call | solution.py:169
  23.8 0.0 all-reduce.3.cloned.1.call-update
  23.8 0.0 all-gather.2.cloned.1.call-start
  23.9 0.0 copy-done.2
  23.9 0.6 dynamic-slice
  25.1 121.6 %all-reduce.3.cloned.1.call-done = f32[256,2688]{1,0:T(8,128)} async-done(((f32[256,2688]{1,0:T(8,128)}), f32[256,2688]{1,0:T(8,128)}) %all-reduce.3.cloned.1.call-update) | async-done | bytes 2752528
  146.7 1.4 constant_dynamic-slice_fusion
  148.1 0.0 all-gather.2.cloned.1.call-update
  148.1 1.5 constant_dynamic-slice_fusion.1.own_ref
  149.7 47.7 %all-gather.2.cloned.1.call-done.gathered_ref = f32[256,1152]{1,0:T(8,128)} async-done(((f32[8,1152]{1,0:T(8,128)}), f32[256,1152]{1,0:T(8,128)}) %all-gather.2.cloned.1.call-update) | async-done | bytes 1179664 | tf_op jit(solution)/shard_map/all_gather | solution.py:285
  197.3 8.2 %level1.1 = (f32[8,1664]{1,0:T(8,128)}, f32[256,896]{1,0:T(8,128)}) custom-call(f32[256,1152]{1,0:T(8,128)} %all-gather.2.cloned.1.call-done.gathered_ref, f32[8,2688]{1,0:T(8,128)} %constant_dynamic-slice_fusion.1.own_ref), custom_call_target="tpu_custom_call" | custom-call | tf_op jit(solution)/shard_map/level1/pallas_call | solution.py:221
  205.5 1.3 collective-permute-start
  206.8 1.9 collective-permute-done
  208.7 0.8 add.11.own_ref
  209.5 0.0 copy-start
  209.6 27.9 %all_gather.13.gathered_ref = f32[256,896]{1,0:T(8,128)} all-gather(f32[8,896]{1,0:T(8,128)S(1)} %slice.16), channel_id=1, replica_groups={{0,1,2,3,4,5,6,7,8,9,10,11,12,13,14,15,16,17,18,19,20,21,22,23,24,25,26..., dimensions={0}, use_global_device_ids=true | all-gather | bytes 946176 | tf_op jit(solution)/shard_map/all_gather | solution.py:285
  237.5 0.0 copy-done
  237.5 7.6 %level2.1 = (f32[8,896]{1,0:T(8,128)}, f32[256,640]{1,0:T(8,128)}) custom-call(f32[256,896]{1,0:T(8,128)} %all_gather.13.gathered_ref, f32[8,1664]{1,0:T(8,128)} %copy-done), custom_call_target="tpu_custom_call" | custom-call | tf_op jit(solution)/shard_map/level2/pallas_call | solution.py:221
  245.1 2.3 collective-permute-start.1
  247.3 1.6 collective-permute-done.1
  248.9 0.8 add.12.own_ref
  249.6 0.0 copy-start.1
  249.7 26.1 %all_gather.14.gathered_ref = f32[256,640]{1,0:T(8,128)} all-gather(f32[8,640]{1,0:T(8,128)S(1)} %slice.17), channel_id=1, replica_groups={{0,1,2,3,4,5,6,7,8,9,10,11,12,13,14,15,16,17,18,19,20,21,22,23,24,25,26..., dimensions={0}, use_global_device_ids=true | all-gather | bytes 675840 | tf_op jit(solution)/shard_map/all_gather | solution.py:285
  275.7 0.0 copy-done.1
  275.7 7.0 %level3.1 = (f32[8,384]{1,0:T(8,128)}, f32[256,384]{1,0:T(8,128)}) custom-call(f32[256,640]{1,0:T(8,128)} %all_gather.14.gathered_ref, f32[8,896]{1,0:T(8,128)} %copy-done.1), custom_call_target="tpu_custom_call" | custom-call | tf_op jit(solution)/shard_map/level3/pallas_call | solution.py:221
  282.7 5.8 %collective-permute-start.2 = (f32[8,384]{1,0:T(8,128)}, f32[8,384]{1,0:T(8,128)S(1)}, u32[]{:S(2)}, u32[]{:S(2)}) collective-permute-start(f32[8,384]{1,0:T(8,128)} %get-tuple-element.17), channel_id=1, source_target_pairs={{0,128},{1,129},{2,130},{3,131},{4,132},{5,133},{6,134},{7,135},{8... | collective-permute-start | bytes 36872 | tf_op jit(solution)/shard_map/ppermute | solution.py:284
  288.5 1.3 collective-permute-done.2
  289.8 0.7 add.13
  290.5 27.2 %all_gather.15.gathered_ref = f32[256,384]{1,0:T(8,128)} all-gather(f32[8,384]{1,0:T(8,128)S(1)} %add.13), channel_id=1, replica_groups={{0,1,2,3,4,5,6,7,8,9,10,11,12,13,14,15,16,17,18,19,20,21,22,23,24,25,26..., dimensions={0}, use_global_device_ids=true | all-gather | bytes 405504 | tf_op jit(solution)/shard_map/all_gather | solution.py:285
  317.6 11.3 %last.1 = f32[8,512]{1,0:T(8,128)} custom-call(f32[256,384]{1,0:T(8,128)} %all_gather.15.gathered_ref, f32[256,896]{1,0:T(8,128)} %get-tuple-element.18.h1_ref, f32[256,640]{1,0:T(8,128)} %get-tuple-element.19.h2_ref, f32[256,384]{1,0:T(8,128)} %get-tuple-element.20.h3_ref, f32[512,512]{1,0:T(8,128)} %get-tuple-element.21.inverse_ref, ...), custom_call_target="tpu_custom_call" | custom-call | tf_op jit(solution)/shard_map/last/pallas_call | solution.py:257
  329.0 1.3 slice.18
  (2 shorter events, 0.0 us)
Async XLA Ops:
  6.5 17.4 %copy-start.2 = (u32[256]{0:T(256)S(1)}, u32[256]{0:T(256)}, u32[]{:S(2)}) copy-start(u32[256]{0:T(256)} %constant.3) | copy-start | bytes 3076
  6.5 140.2 %all-reduce.3.cloned.1.call-start = ((), (), s32[]{:S(2)}) async-start(), calls=%async_computation.1 | async-start | bytes 5505024
  23.8 173.5 %all-gather.2.cloned.1.call-start = ((), (), s32[]{:S(2)}) async-start(), calls=%async_computation | async-start | bytes 1216512 | tf_op jit(solution)/shard_map/all_gather | solution.py:285
  205.5 3.2 collective-permute-start
  209.5 28.0 %copy-start = (f32[8,1664]{1,0:T(8,128)}, f32[8,1664]{1,0:T(8,128)S(1)}, u32[]{:S(2)}) copy-start(f32[8,1664]{1,0:T(8,128)S(1)} %add.11.own_ref) | copy-start | bytes 159748
  245.1 3.8 %collective-permute-start.1 = (f32[8,896]{1,0:T(8,128)}, f32[8,896]{1,0:T(8,128)S(1)}, u32[]{:S(2)}, u32[]{:S(2)}) collective-permute-start(f32[8,896]{1,0:T(8,128)} %get-tuple-element.16), channel_id=1, source_target_pairs={{0,64},{1,65},{2,66},{3,67},{4,68},{5,69},{6,70},{7,71},{8,72},{9,... | collective-permute-start | bytes 86024 | tf_op jit(solution)/shard_map/ppermute | solution.py:284
  249.6 26.1 %copy-start.1 = (f32[8,896]{1,0:T(8,128)}, f32[8,896]{1,0:T(8,128)S(1)}, u32[]{:S(2)}) copy-start(f32[8,896]{1,0:T(8,128)S(1)} %add.12.own_ref) | copy-start | bytes 86020
  282.7 7.1 %collective-permute-start.2 = (f32[8,384]{1,0:T(8,128)}, f32[8,384]{1,0:T(8,128)S(1)}, u32[]{:S(2)}, u32[]{:S(2)}) collective-permute-start(f32[8,384]{1,0:T(8,128)} %get-tuple-element.17), channel_id=1, source_target_pairs={{0,128},{1,129},{2,130},{3,131},{4,132},{5,133},{6,134},{7,135},{8... | collective-permute-start | bytes 36872 | tf_op jit(solution)/shard_map/ppermute | solution.py:284
Sparse Core Ops, SparseCore 0:
  24.0 122.7 all-reduce.2
  149.4 47.9 all-gather.1

commit v2 on v1

--- a/solution.py
+++ b/solution.py
@@ -193,7 +193,7 @@
     h_ref[...] = h
     width = (left - 1) * R
     h_parts = split(h)
-    mine = lax.rem(lax.axis_index("leaf"), PLANE) * 8
+    mine = own_tile() * 8
     wanted = lax.broadcasted_iota(jnp.int32, (8, R), 1) == lax.broadcasted_iota(jnp.int32, (8, R), 0) + mine
     one_hot = jnp.where(wanted, 1.0, 0.0).astype(BF16)
     lane = lax.broadcasted_iota(jnp.int32, (8, LANES), 1)
@@ -265,26 +265,239 @@
     )(gathered, h1, h2, h3, inverse, rows, bases)
 
 
-def planes(count):
-    return [[p * PLANE + d for d in range(PLANE)] for p in range(count)]
+def place():
+    at = lax.axis_index("leaf")
+    return at // PLANE, at // 8 % 4, at // 2 % 4, at % 2
+
+
+def device(plane, x, y, core):
+    return ((plane * 4 + x) * 4 + y) * 2 + core
+
+
+def own_tile():
+    plane, x, y, core = place()
+    return core * 16 + x * 4 + y
+
+
+def along(axis, k):
+    plane, x, y, core = place()
+    if axis == 0:
+        to = (x + k) % 4
+        return device(plane, to, y, core), to
+    to = (y + k) % 4
+    return device(plane, x, to, core), to
+
+
+def partner():
+    plane, x, y, core = place()
+    return device(plane, x, y, 1 - core)
+
+
+def greet(others):
+    barrier = pltpu.get_barrier_semaphore()
+    for other in others:
+        pl.semaphore_signal(barrier, inc=1, device_id=(other,), device_id_type=pl.DeviceIdType.MESH)
+    pl.semaphore_wait(barrier, len(others))
+
+
+def plane_mates():
+    return [partner()] + [along(axis, k)[0] for axis in (0, 1) for k in (1, 2, 3)]
+
+
+def send(source, target, sems, index, to):
+    copy = pltpu.make_async_remote_copy(
+        src_ref=source,
+        dst_ref=target,
+        send_sem=sems[0].at[index],
+        recv_sem=sems[1].at[index],
+        device_id=(to,),
+        device_id_type=pl.DeviceIdType.MESH,
+    )
+    copy.start()
+    return copy
+
+
+def gather(own_ref, gathered_ref, sems, width):
+    plane, x, y, core = place()
+    half = width // 2 // LANES * LANES
+    halves = ((0, slice(0, half)), (1, slice(half, width)))
+    fence = []
+    index = 0
+    first, second = [], []
+    for axis, cols in halves:
+        copies = []
+        for k in (1, 2, 3):
+            to = along(axis, k)[0]
+            copies.append(send(own_ref.at[:, cols], gathered_ref.at[core, x, y, :, cols], sems, index, to))
+            index += 1
+        first.append(copies)
+        gathered_ref[core, x, y, :, cols] = own_ref[:, cols]
+    fence.append(send(own_ref.at[:, 0:width], gathered_ref.at[core, x, y], sems, index, partner()))
+    index += 1
+    for (axis, cols), copies in zip(halves, first):
+        for copy in copies:
+            copy.wait_recv()
+        moved = []
+        for k in (1, 2, 3):
+            to = along(1 - axis, k)[0]
+            if axis == 0:
+                block = gathered_ref.at[core, :, y, :, cols]
+            else:
+                block = gathered_ref.at[core, x, :, :, cols]
+            moved.append(send(block, block, sems, index, to))
+            index += 1
+        for k in (1, 2, 3):
+            at = (along(axis, k)[1], y) if axis == 0 else (x, along(axis, k)[1])
+            block = gathered_ref.at[core, at[0], at[1], :, cols]
+            fence.append(send(block, block, sems, index, partner()))
+            index += 1
+        second.append(moved)
+    for k in (1, 2, 3):
+        for (axis, cols), moved in zip(halves, second):
+            moved[k - 1].wait_recv()
+            if axis == 0:
+                block = gathered_ref.at[core, :, along(1, 4 - k)[1], :, cols]
+            else:
+                block = gathered_ref.at[core, along(0, 4 - k)[1], :, :, cols]
+            fence.append(send(block, block, sems, index, partner()))
+            index += 1
+    for copies in first + second:
+        for copy in copies:
+            copy.wait_send()
+    for copy in fence:
+        copy.wait()
+
+
+GATHER_COPIES = 25
+SPLIT = 11 * LANES
+
+
+def sum_kernel(front_ref, own_ref, gathered_ref, got_ref, a_ref, b_ref, got_a_ref, got_b_ref, a2_ref, b2_ref,
+               got_a2_ref, got_b2_ref, send_sem, recv_sem, gather_send, gather_recv):
+    plane, x, y, core = place()
+    greet(plane_mates())
+    sems = (send_sem, recv_sem)
+    cols = (slice(0, SPLIT), slice(SPLIT, FRONT))
+    other = partner()
+    swaps = [send(front_ref.at[1 - core, :, :, :, c], got_ref.at[:, :, :, c], sems, i, other) for i, c in enumerate(cols)]
+    swaps[0].wait_recv()
+    a_ref[...] = front_ref[core, :, :, :, cols[0]] + got_ref[:, :, :, cols[0]]
+    first_a = []
+    for k in (1, 2, 3):
+        to, at = along(0, k)
+        first_a.append(send(a_ref.at[at], got_a_ref.at[k - 1], sems, 1 + k, to))
+    swaps[1].wait_recv()
+    for i in range(4):
+        b_ref[:, i] = front_ref[core, i, :, :, cols[1]] + got_ref[i, :, :, cols[1]]
+    first_b = []
+    for k in (1, 2, 3):
+        to, at = along(1, k)
+        first_b.append(send(b_ref.at[at], got_b_ref.at[k - 1], sems, 4 + k, to))
+    for copy in first_a:
+        copy.wait_recv()
+    a2_ref[...] = (a_ref[x] + got_a_ref[0]) + (got_a_ref[1] + got_a_ref[2])
+    second_a = []
+    for k in (1, 2, 3):
+        to, at = along(1, k)
+        second_a.append(send(a2_ref.at[at], got_a2_ref.at[k - 1], sems, 7 + k, to))
+    for copy in first_b:
+        copy.wait_recv()
+    b2_ref[...] = (b_ref[y] + got_b_ref[0]) + (got_b_ref[1] + got_b_ref[2])
+    second_b = []
+    for k in (1, 2, 3):
+        to, at = along(0, k)
+        second_b.append(send(b2_ref.at[at], got_b2_ref.at[k - 1], sems, 10 + k, to))
+    for copy in second_a:
+        copy.wait_recv()
+    own_ref[:, cols[0]] = (a2_ref[y] + got_a2_ref[0]) + (got_a2_ref[1] + got_a2_ref[2])
+    for copy in second_b:
+        copy.wait_recv()
+    own_ref[:, cols[1]] = (b2_ref[x] + got_b2_ref[0]) + (got_b2_ref[1] + got_b2_ref[2])
+    gather(own_ref, gathered_ref, (gather_send, gather_recv), gathered_ref.shape[-1])
+    for copy in swaps + first_a + first_b + second_a + second_b:
+        copy.wait_send()
+
+
+def sum_call(front):
+    width = LEVELS * R + LANES
+    rest = FRONT - SPLIT
+    return pl.pallas_call(
+        sum_kernel,
+        out_shape=(
+            jax.ShapeDtypeStruct((8, FRONT), F32),
+            jax.ShapeDtypeStruct((2, 4, 4, 8, width), F32),
+        ),
+        in_specs=vmem(1),
+        out_specs=tuple(vmem(2)),
+        scratch_shapes=[
+            pltpu.VMEM((4, 4, 8, FRONT), F32),
+            pltpu.VMEM((4, 4, 8, SPLIT), F32),
+            pltpu.VMEM((4, 4, 8, rest), F32),
+            pltpu.VMEM((3, 4, 8, SPLIT), F32),
+            pltpu.VMEM((3, 4, 8, rest), F32),
+            pltpu.VMEM((4, 8, SPLIT), F32),
+            pltpu.VMEM((4, 8, rest), F32),
+            pltpu.VMEM((3, 8, SPLIT), F32),
+            pltpu.VMEM((3, 8, rest), F32),
+            pltpu.SemaphoreType.DMA((14,)),
+            pltpu.SemaphoreType.DMA((14,)),
+            pltpu.SemaphoreType.DMA((GATHER_COPIES,)),
+            pltpu.SemaphoreType.DMA((GATHER_COPIES,)),
+        ],
+        compiler_params=pltpu.CompilerParams(
+            vmem_limit_bytes=60 * 1024 * 1024, collective_id=0, has_side_effects=True
+        ),
+        name="sum_gather",
+    )(front.reshape(2, 4, 4, 8, FRONT))
+
+
+def pair_kernel(step, part_ref, own_ref, gathered_ref, got_ref, send_sem, recv_sem, gather_send, gather_recv):
+    plane, x, y, core = place()
+    beyond = plane + step - 2 * step * (plane // step % 2)
+    mate = device(beyond, x, y, core)
+    greet(plane_mates() + [mate])
+    swap = send(part_ref, got_ref, (send_sem, recv_sem), 0, mate)
+    swap.wait()
+    own_ref[...] = part_ref[...] + got_ref[...]
+    gather(own_ref, gathered_ref, (gather_send, gather_recv), gathered_ref.shape[-1])
+
+
+def pair_call(level, part):
+    left = LEVELS - level
+    width = left * R + LANES
+    return pl.pallas_call(
+        functools.partial(pair_kernel, 2 ** (level - 1)),
+        out_shape=(
+            jax.ShapeDtypeStruct(part.shape, F32),
+            jax.ShapeDtypeStruct((2, 4, 4, 8, width), F32),
+        ),
+        in_specs=vmem(1),
+        out_specs=tuple(vmem(2)),
+        scratch_shapes=[
+            pltpu.VMEM(part.shape, F32),
+            pltpu.SemaphoreType.DMA((1,)),
+            pltpu.SemaphoreType.DMA((1,)),
+            pltpu.SemaphoreType.DMA((GATHER_COPIES,)),
+            pltpu.SemaphoreType.DMA((GATHER_COPIES,)),
+        ],
+        compiler_params=pltpu.CompilerParams(
+            vmem_limit_bytes=60 * 1024 * 1024, collective_id=level, has_side_effects=True
+        ),
+        name=f"pair_gather{level}",
+    )(part)
 
 
 def local(coords, latent, labels, site_order, level_bases):
-    count = lax.axis_size("leaf")
-    groups = planes(count // PLANE)
     front, inverse, rows = leaf_call(
         coords, latent.reshape(1, M), labels.reshape(1, M), site_order, level_bases
     )
-    own = lax.psum_scatter(front, "leaf", axis_index_groups=groups, scatter_dimension=0, tiled=True)
+    own, gathered = sum_call(front)
     h = []
     for level in range(LEVELS):
         left = LEVELS - level
         if level > 0:
-            bit = PLANE << (level - 1)
-            own = own + lax.ppermute(own, "leaf", [(d, d ^ bit) for d in range(count)])
-        gathered = lax.all_gather(
-            own[:, :left * R + LANES], "leaf", axis_index_groups=groups, axis=0, tiled=True
-        )
+            own, gathered = pair_call(level, own)
+        gathered = gathered.reshape(R, left * R + LANES)
         if left > 1:
             own, part = level_call(left, gathered, own)
             h.append(part)

time: 337 us -> 144 us (0.43)
  waiting for transfers between devices: 174 us -> 0 us
  Pallas kernels: 51.3 us -> 142 us
  blocking collectives: 81.2 us -> 0 us
  between operations: 14.1 us -> 0.04 us
  starting transfers between devices: 9.35 us -> 0 us
  local copies, waits for them, and re-layouts: 4.81 us -> 1.3 us
    unnamed x3 -> x0, waiting for transfers between devices: 122 us -> none
    pallas_call x0 -> x4, Pallas kernels: none -> 91.1 us  [the longest x3 54.7 us: pair_call(): pl.pallas_call(functools.partial(pair_kernel, 2 ** (level - 1)), out_shap...]
    all_gather x3 -> x0, blocking collectives: 81.2 us -> none  [local(): lax.all_gather(own[:, :left * R + LANES], 'leaf', axis_index_groups=group...]
    all_gather x1 -> x0, waiting for transfers between devices: 47.7 us -> none  [local(): lax.all_gather(own[:, :left * R + LANES], 'leaf', axis_index_groups=group...]
    ppermute x3 -> x0, starting transfers between devices: 9.31 us -> none  [local(): own = own + lax.ppermute(own, 'leaf', [(d, d ^ bit) for d in range(count)])]
    ppermute x3 -> x0, waiting for transfers between devices: 4.78 us -> none  [local(): own = own + lax.ppermute(own, 'leaf', [(d, d ^ bit) for d in range(count)])]
  transfers between devices with their start and end apart: 5 -> 0, of which waited for: 5 -> 0; matrix products, arithmetic and copies ran while one was open for 1% -> 0% of each run, Pallas kernels for 0% -> 0%
where the time goes in v2:
time: 144 us
  Pallas kernels  142 us (99%)
    pallas_call x3, Pallas kernels, pair_call(): pl.pallas_call(functools.partial(pair_kernel, 2 ** (level - 1)), out_shap...  54.7 us
    pallas_call x1, Pallas kernels, sum_call(): pl.pallas_call(sum_kernel, out_shape=(jax.ShapeDtypeStruct((8, FRONT), F3...  36.4 us
    pallas_call x3, Pallas kernels, level_call(): pl.pallas_call(functools.partial(level_kernel, left), out_shape=(jax.Shap...  23 us
    pallas_call x1, Pallas kernels, leaf_call(): pl.pallas_call(leaf_kernel, out_shape=(jax.ShapeDtypeStruct((R, FRONT), F...  17.2 us
    pallas_call x1, Pallas kernels, last_call(): pl.pallas_call(last_kernel, out_shape=jax.ShapeDtypeStruct((8, M), F32),...  11.1 us

profile of v2, /device:TPU:1, one launch (start us, length us, event | category | flops | bytes accessed | tf_op | source)
XLA Modules:
  0.0 143.7 jit_solution(13452613244775807398)
XLA Ops:
  0.0 17.2 %leaf.1 = (f32[256,2688]{1,0:T(8,128)}, f32[512,512]{1,0:T(8,128)}, f32[8,512]{1,0:T(8,128)}) custom-call(f32[3,512]{1,0:T(4,128)} %coord_ref.1, f32[1,512]{1,0:T(1,128)} %bitcast.13, s32[1,512]{1,0:T(1,128)} %bitcast.14, s32[1,512]{1,0:T(1,128)} %order_ref.1, bf16[4,256,512]{2,1,0:T(8,128)(2,1)} %basis_ref.3), custom_call_target="tpu_custom_call" | custom-call | tf_op jit(solution)/shard_map/leaf/pallas_call | solution.py:169
  17.2 36.4 %sum_gather.1 = (f32[8,2688]{1,0:T(8,128)}, f32[2,4,4,8,1152]{4,3,2,1,0:T(8,128)}) custom-call(f32[2,4,4,8,2688]{4,3,2,1,0:T(8,128)} %bitcast.8), custom_call_target="tpu_custom_call" | custom-call | tf_op jit(solution)/shard_map/sum_gather/pallas_call | solution.py:424
  53.6 8.2 %level1.1 = (f32[8,1664]{1,0:T(8,128)}, f32[256,896]{1,0:T(8,128)}) custom-call(f32[256,1152]{1,0:T(8,128)} %bitcast.9, f32[8,2688]{1,0:T(8,128)} %get-tuple-element.23.own_ref), custom_call_target="tpu_custom_call" | custom-call | tf_op jit(solution)/shard_map/level1/pallas_call | solution.py:221
  61.8 17.6 %pair_gather1.1 = (f32[8,1664]{1,0:T(8,128)}, f32[2,4,4,8,896]{4,3,2,1,0:T(8,128)}) custom-call(f32[8,1664]{1,0:T(8,128)} %get-tuple-element.24.part_ref), custom_call_target="tpu_custom_call" | custom-call | tf_op jit(solution)/shard_map/pair_gather1/pallas_call | solution.py:468
  79.4 7.7 %level2.1 = (f32[8,896]{1,0:T(8,128)}, f32[256,640]{1,0:T(8,128)}) custom-call(f32[256,896]{1,0:T(8,128)} %bitcast.10, f32[8,1664]{1,0:T(8,128)} %get-tuple-element.26.own_ref), custom_call_target="tpu_custom_call" | custom-call | tf_op jit(solution)/shard_map/level2/pallas_call | solution.py:221
  87.2 17.8 %pair_gather2.1 = (f32[8,896]{1,0:T(8,128)}, f32[2,4,4,8,640]{4,3,2,1,0:T(8,128)}) custom-call(f32[8,896]{1,0:T(8,128)} %get-tuple-element.27.part_ref), custom_call_target="tpu_custom_call" | custom-call | tf_op jit(solution)/shard_map/pair_gather2/pallas_call | solution.py:468
  104.9 7.0 %level3.1 = (f32[8,384]{1,0:T(8,128)}, f32[256,384]{1,0:T(8,128)}) custom-call(f32[256,640]{1,0:T(8,128)} %bitcast.11, f32[8,896]{1,0:T(8,128)} %get-tuple-element.29.own_ref), custom_call_target="tpu_custom_call" | custom-call | tf_op jit(solution)/shard_map/level3/pallas_call | solution.py:221
  111.9 19.4 %pair_gather3.1 = (f32[8,384]{1,0:T(8,128)}, f32[2,4,4,8,384]{4,3,2,1,0:T(8,128)}) custom-call(f32[8,384]{1,0:T(8,128)} %get-tuple-element.30.part_ref), custom_call_target="tpu_custom_call" | custom-call | tf_op jit(solution)/shard_map/pair_gather3/pallas_call | solution.py:468
  131.3 11.1 %last.1 = f32[8,512]{1,0:T(8,128)} custom-call(f32[256,384]{1,0:T(8,128)} %bitcast.12, f32[256,896]{1,0:T(8,128)} %get-tuple-element.32.h1_ref, f32[256,640]{1,0:T(8,128)} %get-tuple-element.33.h2_ref, f32[256,384]{1,0:T(8,128)} %get-tuple-element.34.h3_ref, f32[512,512]{1,0:T(8,128)} %get-tuple-element.35.inverse_ref, f32[8,512]{1,0:T(8,128)} %get-tuple-element.36.rows_ref, ...), custom_call_target="tpu_custom_call" | custom-call | tf_op jit(solution)/shard_map/last/pallas_call | solution.py:257
  142.4 1.3 slice.4

commit v3 on v1

--- a/solution.py
+++ b/solution.py
@@ -47,6 +47,22 @@
     return dot(a[0], b[0], dims) + (dot(a[0], b[1], dims) + dot(a[1], b[0], dims))
 
 
+def packed_rows(v):
+    row = lax.broadcasted_iota(jnp.int32, (16, v.shape[1]), 0)
+    out = jnp.zeros((16, v.shape[1]), F32)
+    for i, part in enumerate(split3(v)):
+        out = jnp.where(row == i, part.astype(F32), out)
+    return out.astype(BF16)
+
+
+def row_dot(v, parts, dims=NN):
+    rows = packed_rows(v)
+    total = dot(rows, parts[0], dims)
+    for part in parts[1:]:
+        total = total + dot(rows, part, dims)
+    return (total[0:1] + total[1:2]) + total[2:3]
+
+
 def eye(n):
     return jnp.where(
         lax.broadcasted_iota(jnp.int32, (n, n), 0) == lax.broadcasted_iota(jnp.int32, (n, n), 1), 1.0, 0.0
@@ -77,8 +93,8 @@
     return z + dot3(split(z), split(residual))
 
 
-def leaf_kernel(coord_ref, latent_ref, label_ref, order_ref, basis_ref, front_ref, inverse_ref, rows_ref,
-                a_ref, z_ref, mh_ref, ml_ref):
+def leaf_kernel(coord_ref, latent_ref, label_ref, order_ref, basis_ref, mh_ref, ml_ref, tile_ref,
+                inverse_ref, rows_ref, a_ref, z_ref):
     picked = lax.broadcasted_iota(jnp.int32, (M, M), 0) == order_ref[...]
     one_hot = jnp.where(picked, 1.0, 0.0).astype(BF16)
     hi, mid, lo = split3(latent_ref[...])
@@ -136,23 +152,15 @@
             hi, lo = split(columns[i] * inverse_ref[rows, span] * root_weight[:, span])
             mh_ref[rows, span] = hi
             ml_ref[rows, span] = lo
-    solved = dot_f32(jnp.broadcast_to(right_side, (8, M)), inverse_ref[...])[0:1]
+    solved = row_dot(right_side, split3(inverse_ref[...]))
     weighted = split3(root_weight * solved)
     lane = lax.broadcasted_iota(jnp.int32, (LANES, M), 0)
     tile = jnp.zeros((R, LANES), F32)
-    offset = 0
     for level in range(LEVELS):
-        basis = basis_ref[level]
-        part = split(dot(basis, mh_ref[...]) + dot(basis, ml_ref[...]))
-        for other in range(level, LEVELS):
-            front_ref[:, offset:offset + R] = dot(part[0], basis_ref[other], NT) + dot(part[1], basis_ref[other], NT)
-            offset += R
-        if level == 0:
-            offset += LANES
         for piece in weighted:
             placed = jnp.where(lane == level, piece.astype(F32), 0.0).astype(BF16)
-            tile = tile + dot(basis, placed, NT)
-    front_ref[:, LEVELS * R:LEVELS * R + LANES] = tile
+            tile = tile + dot(basis_ref[level], placed, NT)
+    tile_ref[...] = tile
     row = lax.broadcasted_iota(jnp.int32, (8, M), 0)
     rows_ref[...] = jnp.where(row == 0, root_weight, right_side)
 
@@ -169,39 +177,51 @@
     return pl.pallas_call(
         leaf_kernel,
         out_shape=(
-            jax.ShapeDtypeStruct((R, FRONT), F32),
+            jax.ShapeDtypeStruct((M, M), BF16),
+            jax.ShapeDtypeStruct((M, M), BF16),
+            jax.ShapeDtypeStruct((R, LANES), F32),
             jax.ShapeDtypeStruct((M, M), F32),
             jax.ShapeDtypeStruct((8, M), F32),
         ),
         in_specs=vmem(5),
-        out_specs=tuple(vmem(3)),
-        scratch_shapes=[
-            pltpu.VMEM((M, M), F32), pltpu.VMEM((R, R), F32), pltpu.VMEM((M, M), BF16), pltpu.VMEM((M, M), BF16)
-        ],
+        out_specs=tuple(vmem(5)),
+        scratch_shapes=[pltpu.VMEM((M, M), F32), pltpu.VMEM((R, R), F32)],
         compiler_params=PARAMS,
         name="leaf",
     )(coords, latent, labels, order, bases)
 
 
-def eliminate(left, gathered_ref, z_ref):
-    inverse = newton_inverse(gathered_ref[:, 0:R] + eye(R), z_ref)
-    return dot3(split(inverse), split(gathered_ref[:, R:left * R + LANES]))
-
-
-def level_kernel(left, gathered_ref, own_ref, next_ref, h_ref, z_ref):
-    h = eliminate(left, gathered_ref, z_ref)
+def inverse_kernel(gathered_ref, inverse_ref, z_ref):
+    inverse_ref[...] = newton_inverse(gathered_ref[...] + eye(R), z_ref)
+
+
+def inverse_call(gathered):
+    return pl.pallas_call(
+        inverse_kernel,
+        grid=(1,),
+        out_shape=jax.ShapeDtypeStruct((R, R), F32),
+        in_specs=[pl.BlockSpec((R, R), lambda i: (0, 0))],
+        out_specs=pl.BlockSpec((R, R), lambda i: (0, 0)),
+        scratch_shapes=[pltpu.VMEM((R, R), F32)],
+        compiler_params=PARAMS,
+        name="inverse",
+    )(gathered)
+
+
+def eliminate(left, inverse_ref, gathered_ref, own_ref, next_ref, h_ref):
+    h = dot3(split(inverse_ref[...]), split(gathered_ref[:, R:left * R + LANES]))
     h_ref[...] = h
     width = (left - 1) * R
     h_parts = split(h)
-    mine = lax.rem(lax.axis_index("leaf"), PLANE) * 8
+    mine = own_tile() * 8
     wanted = lax.broadcasted_iota(jnp.int32, (8, R), 1) == lax.broadcasted_iota(jnp.int32, (8, R), 0) + mine
     one_hot = jnp.where(wanted, 1.0, 0.0).astype(BF16)
     lane = lax.broadcasted_iota(jnp.int32, (8, LANES), 1)
     tile = own_ref[:, left * R:left * R + LANES]
     source, target = left * R + LANES, 0
     for k in range(1, left):
-        block = split3(gathered_ref[:, k * R:(k + 1) * R])
-        rows = dot(one_hot, block[0], NT) + dot(one_hot, block[1], NT) + dot(one_hot, block[2], NT)
+        block = split(gathered_ref[:, k * R:(k + 1) * R])
+        rows = dot(one_hot, block[0], NT) + dot(one_hot, block[1], NT)
         drop = dot3(split(rows), h_parts)
         span = (left - k) * R
         next_ref[:, target:target + span] = own_ref[:, source:source + span] - drop[:, (k - 1) * R:width]
@@ -217,78 +237,367 @@
     return LANES + R * (left * (left + 1) // 2)
 
 
-def level_call(left, gathered, own):
-    return pl.pallas_call(
-        functools.partial(level_kernel, left),
-        out_shape=(
-            jax.ShapeDtypeStruct((8, own_width(left - 1)), F32),
-            jax.ShapeDtypeStruct((R, (left - 1) * R + LANES), F32),
-        ),
-        in_specs=vmem(2),
-        out_specs=tuple(vmem(2)),
-        scratch_shapes=[pltpu.VMEM((R, R), F32)],
-        compiler_params=PARAMS,
-        name=f"level{LEVELS - left + 1}",
-    )(gathered, own)
-
-
-def last_kernel(gathered_ref, h1_ref, h2_ref, h3_ref, inverse_ref, rows_ref, basis_ref, out_ref, z_ref):
-    h4 = eliminate(1, gathered_ref, z_ref)
+def last_kernel(gathered_ref, h1_any, h2_any, h3_any, inverse_any, basis_any, rows_ref, out_ref,
+                z_ref, h1_ref, h2_ref, h3_ref, inverse_ref, basis_ref, sems):
+    copies = [
+        pltpu.make_async_copy(source, target, sems.at[i])
+        for i, (source, target) in enumerate(
+            ((h3_any, h3_ref), (h2_any, h2_ref), (h1_any, h1_ref), (inverse_any, inverse_ref), (basis_any, basis_ref))
+        )
+    ]
+    for copy in copies:
+        copy.start()
+    inverse = newton_inverse(gathered_ref[:, 0:R] + eye(R), z_ref)
+    h4 = dot3(split(inverse), split(gathered_ref[:, R:R + LANES]))
+    for copy in copies:
+        copy.wait()
+    h_refs = (h1_ref, h2_ref, h3_ref)
+    rows = [h_refs[i][:, (3 - i) * R:(3 - i) * R + LANES].T[i:i + 1, :] for i in range(3)] + [h4.T[3:4, :]]
     total = jnp.zeros((16, M), F32)
-    later = []
     for level in reversed(range(LEVELS)):
-        rest = LEVELS - 1 - level
-        h_ref = (h1_ref, h2_ref, h3_ref, None)[level]
-        tile = h4 if h_ref is None else h_ref[:, rest * R:rest * R + LANES]
-        z = jnp.broadcast_to(tile.T[level:level + 1, :], (8, R))
-        for k, done in enumerate(later):
-            z = z - dot_f32(done, h_ref[:, k * R:(k + 1) * R], NT)
-        later.insert(0, z)
-        hi, mid, lo = split3(z[0:1])
-        row = lax.broadcasted_iota(jnp.int32, (16, R), 0)
-        packed = jnp.where(row == 0, hi.astype(F32), jnp.where(row == 1, mid.astype(F32), jnp.where(row == 2, lo.astype(F32), 0.0)))
-        total = total + dot(packed.astype(BF16), basis_ref[level])
+        z = packed_rows(rows[level])
+        total = total + dot(z, basis_ref[level])
+        for i in range(level):
+            at = (level - i - 1) * R
+            parts = split(h_refs[i][:, at:at + R])
+            drop = dot(z, parts[0], NT) + dot(z, parts[1], NT)
+            rows[i] = rows[i] - ((drop[0:1] + drop[1:2]) + drop[2:3])
     spread = (total[0:1] + total[1:2]) + total[2:3]
-    right = rows_ref[1:2] - rows_ref[0:1] * spread
-    out_ref[...] = dot_f32(jnp.broadcast_to(right, (8, M)), inverse_ref[...])
+    out_ref[...] = row_dot(rows_ref[1:2] - rows_ref[0:1] * spread, split3(inverse_ref[...]))
 
 
 def last_call(gathered, h1, h2, h3, inverse, rows, bases):
+    kept = (h1, h2, h3, inverse, bases)
     return pl.pallas_call(
         last_kernel,
-        out_shape=jax.ShapeDtypeStruct((8, M), F32),
-        in_specs=vmem(7),
+        out_shape=jax.ShapeDtypeStruct((1, M), F32),
+        in_specs=vmem(1) + [pl.BlockSpec(memory_space=pl.ANY)] * 5 + vmem(1),
         out_specs=vmem(1)[0],
-        scratch_shapes=[pltpu.VMEM((R, R), F32)],
+        scratch_shapes=[pltpu.VMEM((R, R), F32)]
+        + [pltpu.VMEM(array.shape, array.dtype) for array in kept]
+        + [pltpu.SemaphoreType.DMA((5,))],
         compiler_params=PARAMS,
         name="last",
-    )(gathered, h1, h2, h3, inverse, rows, bases)
-
-
-def planes(count):
-    return [[p * PLANE + d for d in range(PLANE)] for p in range(count)]
+    )(gathered, *kept, rows)
+
+
+def place():
+    at = lax.axis_index("leaf")
+    return at // PLANE, at // 8 % 4, at // 2 % 4, at % 2
+
+
+def device(plane, x, y, core):
+    return ((plane * 4 + x) * 4 + y) * 2 + core
+
+
+def own_tile():
+    plane, x, y, core = place()
+    return core * 16 + x * 4 + y
+
+
+def along(axis, k):
+    plane, x, y, core = place()
+    if axis == 0:
+        to = (x + k) % 4
+        return device(plane, to, y, core), to
+    to = (y + k) % 4
+    return device(plane, x, to, core), to
+
+
+def partner():
+    plane, x, y, core = place()
+    return device(plane, x, y, 1 - core)
+
+
+def greet(others):
+    barrier = pltpu.get_barrier_semaphore()
+    for other in others:
+        pl.semaphore_signal(barrier, inc=1, device_id=(other,), device_id_type=pl.DeviceIdType.MESH)
+
+
+def meet(others):
+    pl.semaphore_wait(pltpu.get_barrier_semaphore(), len(others))
+
+
+def plane_mates():
+    return [partner()] + [along(axis, k)[0] for axis in (0, 1) for k in (1, 2, 3)]
+
+
+def send(source, target, sems, index, to):
+    copy = pltpu.make_async_remote_copy(
+        src_ref=source,
+        dst_ref=target,
+        send_sem=sems[0].at[index],
+        recv_sem=sems[1].at[index],
+        device_id=(to,),
+        device_id_type=pl.DeviceIdType.MESH,
+    )
+    copy.start()
+    return copy
+
+
+class Gather:
+    def __init__(self, own_ref, gathered_ref, sems):
+        width = gathered_ref.shape[-1]
+        half = width // 2 // LANES * LANES
+        self.own, self.out, self.sems = own_ref, gathered_ref, sems
+        self.halves = ((0, slice(0, half)), (1, slice(half, width)))
+        self.width, self.index, self.fence = width, 0, []
+        self.first, self.second = [], []
+
+    def send(self, source, target, to):
+        self.index += 1
+        return send(source, target, self.sems, self.index - 1, to)
+
+    def share(self, block):
+        self.fence.append(self.send(block, block, partner()))
+
+    def start(self):
+        plane, x, y, core = place()
+        for axis, cols in self.halves:
+            self.first.append([
+                self.send(self.own.at[:, cols], self.out.at[core, x, y, :, cols], along(axis, k)[0])
+                for k in (2, 1, 3)
+            ])
+        whole = slice(0, self.width)
+        self.fence.append(self.send(self.own.at[:, whole], self.out.at[core, x, y], partner()))
+        self.out[core, x, y] = self.own[:, whole]
+
+    def turn(self):
+        plane, x, y, core = place()
+        for (axis, cols), copies in zip(self.halves, self.first):
+            for copy in copies:
+                copy.wait_recv()
+            if axis == 0:
+                block = self.out.at[core, :, y, :, cols]
+            else:
+                block = self.out.at[core, x, :, :, cols]
+            self.second.append([self.send(block, block, along(1 - axis, k)[0]) for k in (2, 1, 3)])
+        for axis, cols in self.halves:
+            for k in (1, 2, 3):
+                at = (along(axis, k)[1], y) if axis == 0 else (x, along(axis, k)[1])
+                self.share(self.out.at[core, at[0], at[1], :, cols])
+
+    def finish(self):
+        plane, x, y, core = place()
+        for i, k in ((1, 1), (2, 3), (0, 2)):
+            for (axis, cols), moved in zip(self.halves, self.second):
+                moved[i].wait_recv()
+                if axis == 0:
+                    self.share(self.out.at[core, :, along(1, 4 - k)[1], :, cols])
+                else:
+                    self.share(self.out.at[core, along(0, 4 - k)[1], :, :, cols])
+
+    def close(self):
+        for copies in self.first + self.second:
+            for copy in copies:
+                copy.wait_send()
+        for copy in self.fence:
+            copy.wait()
+
+
+class Scatter:
+    def __init__(self, mine, got, a, b, got_a, got_b, a2, b2, got_a2, got_b2, sems):
+        self.mine, self.got, self.a, self.b, self.got_a, self.got_b = mine, got, a, b, got_a, got_b
+        self.a2, self.b2, self.got_a2, self.got_b2, self.sems = a2, b2, got_a2, got_b2, sems
+        split_at = a.shape[-1]
+        self.cols = (slice(0, split_at), slice(split_at, mine.shape[-1]))
+        self.all = []
+
+    def spread(self, source, target, axis, index):
+        copies = []
+        for k in (2, 1, 3):
+            to, at = along(axis, k)
+            copies.append(send(source.at[at], target.at[k - 1], self.sems, index + k - 1, to))
+        self.all += copies
+        return copies
+
+    def swap(self, theirs):
+        self.swaps = [
+            send(theirs.at[:, :, :, c], self.got.at[:, :, :, c], self.sems, i, partner()) for i, c in enumerate(self.cols)
+        ]
+        self.all += self.swaps
+
+    def first(self):
+        self.swaps[0].wait_recv()
+        self.a[...] = self.mine[:, :, :, self.cols[0]] + self.got[:, :, :, self.cols[0]]
+        self.first_a = self.spread(self.a, self.got_a, 0, 2)
+        self.swaps[1].wait_recv()
+        for i in range(4):
+            self.b[:, i] = self.mine[i, :, :, self.cols[1]] + self.got[i, :, :, self.cols[1]]
+        self.first_b = self.spread(self.b, self.got_b, 1, 5)
+
+    def second(self):
+        plane, x, y, core = place()
+        for copy in self.first_a:
+            copy.wait_recv()
+        self.a2[...] = (self.a[x] + self.got_a[0]) + (self.got_a[1] + self.got_a[2])
+        self.second_a = self.spread(self.a2, self.got_a2, 1, 8)
+        for copy in self.first_b:
+            copy.wait_recv()
+        self.b2[...] = (self.b[y] + self.got_b[0]) + (self.got_b[1] + self.got_b[2])
+        self.second_b = self.spread(self.b2, self.got_b2, 0, 11)
+
+    def finish(self, own_ref, offset):
+        plane, x, y, core = place()
+        cut, end = offset + self.cols[0].stop, offset + self.cols[1].stop
+        for copy in self.second_a:
+            copy.wait_recv()
+        own_ref[:, offset:cut] = (self.a2[y] + self.got_a2[0]) + (self.got_a2[1] + self.got_a2[2])
+        for copy in self.second_b:
+            copy.wait_recv()
+        own_ref[:, cut:end] = (self.b2[x] + self.got_b2[0]) + (self.got_b2[1] + self.got_b2[2])
+
+    def close(self):
+        for copy in self.all:
+            copy.wait_send()
+
+
+GATHER_COPIES = 25
+HEAD = LEVELS * R + LANES
+TAIL = FRONT - HEAD
+HEAD_CUT = 5 * LANES
+TAIL_CUT = 6 * LANES
+TILES = (4, 4, 8)
+
+
+def scatter_scratch(width, cut):
+    rest = width - cut
+    shapes = [
+        TILES + (width,), TILES + (width,), TILES + (width,), TILES + (cut,), TILES + (rest,), (3, 4, 8, cut),
+        (3, 4, 8, rest), (4, 8, cut), (4, 8, rest), (3, 8, cut), (3, 8, rest),
+    ]
+    return [pltpu.VMEM(shape, F32) for shape in shapes] + [pltpu.SemaphoreType.DMA((14,))] * 2
+
+
+def sum_kernel(mh_ref, ml_ref, tile_ref, basis_ref, own_ref, gathered_ref, *scratch):
+    plane, x, y, core = place()
+    mates = plane_mates()
+    greet(mates)
+
+    def grams(half, level, target, offset):
+        basis = basis_ref[level, pl.ds(pl.multiple_of(half * LANES, LANES), LANES), :]
+        part = split(dot(basis, mh_ref[...]) + dot(basis, ml_ref[...]))
+        for other in range(level, LEVELS):
+            block = dot(part[0], basis_ref[other], NT) + dot(part[1], basis_ref[other], NT)
+            target[:, :, :, offset:offset + R] = block.reshape(TILES + (R,))
+            offset += R
+        if level == 0:
+            tile = tile_ref[pl.ds(pl.multiple_of(half * LANES, LANES), LANES), :]
+            target[:, :, :, offset:offset + LANES] = tile.reshape(TILES + (LANES,))
+
+    def tail(half, target):
+        grams(half, 1, target, 0)
+        grams(half, 2, target, 3 * R)
+        grams(half, 3, target, 5 * R)
+
+    theirs0, mine0, theirs1, mine1 = scratch[0], scratch[1], scratch[13], scratch[14]
+    head_sum = Scatter(*scratch[1:11], scratch[11:13])
+    tail_sum = Scatter(*scratch[14:24], scratch[24:26])
+    gather = Gather(own_ref, gathered_ref, scratch[26:28])
+    grams(1 - core, 0, theirs0, 0)
+    meet(mates)
+    head_sum.swap(theirs0)
+    grams(core, 0, mine0, 0)
+    head_sum.first()
+    tail(1 - core, theirs1)
+    tail_sum.swap(theirs1)
+    tail(core, mine1)
+    head_sum.second()
+    tail_sum.first()
+    head_sum.finish(own_ref, 0)
+    gather.start()
+    gather.turn()
+    tail_sum.second()
+    gather.finish()
+    tail_sum.finish(own_ref, HEAD)
+    gather.close()
+    head_sum.close()
+    tail_sum.close()
+
+
+def sum_call(mh, ml, tile, bases):
+    return pl.pallas_call(
+        sum_kernel,
+        out_shape=(
+            jax.ShapeDtypeStruct((8, FRONT), F32),
+            jax.ShapeDtypeStruct((2,) + TILES + (HEAD,), F32),
+        ),
+        in_specs=vmem(4),
+        out_specs=tuple(vmem(2)),
+        scratch_shapes=scatter_scratch(HEAD, HEAD_CUT)
+        + scatter_scratch(TAIL, TAIL_CUT)
+        + [pltpu.SemaphoreType.DMA((GATHER_COPIES,))] * 2,
+        compiler_params=pltpu.CompilerParams(
+            vmem_limit_bytes=60 * 1024 * 1024, collective_id=0, has_side_effects=True
+        ),
+        name="sum_gather",
+    )(mh, ml, tile, bases)
+
+
+def pair_kernel(level, inverse_ref, before_ref, had_ref, own_ref, gathered_ref, h_ref, part_ref, got_ref,
+                send_sem, recv_sem, gather_send, gather_recv):
+    plane, x, y, core = place()
+    step = 2 ** (level - 1)
+    if level == LEVELS - 1:
+        beyond = 2 * step - 1 - plane
+    else:
+        beyond = plane + step - 2 * step * (plane // step % 2)
+    mates = plane_mates() + [device(beyond, x, y, core)]
+    greet(mates)
+    eliminate(LEVELS - level + 1, inverse_ref, before_ref, had_ref, part_ref, h_ref)
+    meet(mates)
+    swap = send(part_ref, got_ref, (send_sem, recv_sem), 0, mates[-1])
+    swap.wait_recv()
+    own_ref[...] = part_ref[...] + got_ref[...]
+    gather = Gather(own_ref, gathered_ref, (gather_send, gather_recv))
+    gather.start()
+    gather.turn()
+    gather.finish()
+    gather.close()
+    swap.wait_send()
+
+
+def pair_call(level, inverse, gathered, own):
+    left = LEVELS - level
+    width = left * R + LANES
+    slab = (8, own_width(left))
+    return pl.pallas_call(
+        functools.partial(pair_kernel, level),
+        out_shape=(
+            jax.ShapeDtypeStruct(slab, F32),
+            jax.ShapeDtypeStruct((2,) + TILES + (width,), F32),
+            jax.ShapeDtypeStruct((R, width), F32),
+        ),
+        in_specs=vmem(3),
+        out_specs=tuple(vmem(3)),
+        scratch_shapes=[
+            pltpu.VMEM(slab, F32),
+            pltpu.VMEM(slab, F32),
+            pltpu.SemaphoreType.DMA((1,)),
+            pltpu.SemaphoreType.DMA((1,)),
+            pltpu.SemaphoreType.DMA((GATHER_COPIES,)),
+            pltpu.SemaphoreType.DMA((GATHER_COPIES,)),
+        ],
+        compiler_params=pltpu.CompilerParams(
+            vmem_limit_bytes=60 * 1024 * 1024, collective_id=level, has_side_effects=True
+        ),
+        name=f"pair_gather{level}",
+    )(inverse, gathered, own)
 
 
 def local(coords, latent, labels, site_order, level_bases):
-    count = lax.axis_size("leaf")
-    groups = planes(count // PLANE)
-    front, inverse, rows = leaf_call(
+    mh, ml, tile, inverse, rows = leaf_call(
         coords, latent.reshape(1, M), labels.reshape(1, M), site_order, level_bases
     )
-    own = lax.psum_scatter(front, "leaf", axis_index_groups=groups, scatter_dimension=0, tiled=True)
+    own, gathered = sum_call(mh, ml, tile, level_bases)
+    gathered = gathered.reshape(R, HEAD)
     h = []
-    for level in range(LEVELS):
-        left = LEVELS - level
-        if level > 0:
-            bit = PLANE << (level - 1)
-            own = own + lax.ppermute(own, "leaf", [(d, d ^ bit) for d in range(count)])
-        gathered = lax.all_gather(
-            own[:, :left * R + LANES], "leaf", axis_index_groups=groups, axis=0, tiled=True
-        )
-        if left > 1:
-            own, part = level_call(left, gathered, own)
-            h.append(part)
-    return last_call(gathered, *h, inverse, rows, level_bases)[0]
+    for level in range(1, LEVELS):
+        own, after, part = pair_call(level, inverse_call(gathered), gathered, own)
+        h.append(part)
+        gathered = after.reshape(R, (LEVELS - level) * R + LANES)
+    return last_call(gathered, *h, inverse, rows, level_bases).reshape(M)
 
 
 def solution(mesh):

time: 337 us -> 128 us (0.38)
  waiting for transfers between devices: 174 us -> 0 us
  blocking collectives: 81.2 us -> 0 us
  Pallas kernels: 51.3 us -> 128 us
  between operations: 14.1 us -> 0.2 us
  starting transfers between devices: 9.35 us -> 0 us
  local copies, waits for them, and re-layouts: 4.81 us -> 0 us
    unnamed x3 -> x0, waiting for transfers between devices: 122 us -> none
    all_gather x3 -> x0, blocking collectives: 81.2 us -> none  [local(): lax.all_gather(own[:, :left * R + LANES], 'leaf', axis_index_groups=group...]
    pallas_call x5 -> x9, Pallas kernels: 51.3 us -> 128 us  [the longest x3 54.2 us: pair_call(): pl.pallas_call(functools.partial(pair_kernel, level), out_shape=(jax.Shap...]
    all_gather x1 -> x0, waiting for transfers between devices: 47.7 us -> none  [local(): lax.all_gather(own[:, :left * R + LANES], 'leaf', axis_index_groups=group...]
    ppermute x3 -> x0, starting transfers between devices: 9.31 us -> none  [local(): own = own + lax.ppermute(own, 'leaf', [(d, d ^ bit) for d in range(count)])]
    ppermute x3 -> x0, waiting for transfers between devices: 4.78 us -> none  [local(): own = own + lax.ppermute(own, 'leaf', [(d, d ^ bit) for d in range(count)])]
  transfers between devices with their start and end apart: 5 -> 0, of which waited for: 5 -> 0; matrix products, arithmetic and copies ran while one was open for 1% -> 0% of each run, Pallas kernels for 0% -> 0%
where the time goes in v3:
time: 128 us
  Pallas kernels  128 us (100%)
    pallas_call x3, Pallas kernels, pair_call(): pl.pallas_call(functools.partial(pair_kernel, level), out_shape=(jax.Shap...  54.2 us
    pallas_call x1, Pallas kernels, sum_call(): pl.pallas_call(sum_kernel, out_shape=(jax.ShapeDtypeStruct((8, FRONT), F3...  32.3 us
    pallas_call x3, Pallas kernels, inverse_call(): pl.pallas_call(inverse_kernel, grid=(1,), out_shape=jax.ShapeDtypeStruct(...  18.5 us
    pallas_call x1, Pallas kernels, leaf_call(): pl.pallas_call(leaf_kernel, out_shape=(jax.ShapeDtypeStruct((M, M), BF16)...  14 us
    pallas_call x1, Pallas kernels, last_call(): pl.pallas_call(last_kernel, out_shape=jax.ShapeDtypeStruct((1, M), F32),...  8.6 us

profile of v3, /device:TPU:1, one launch (start us, length us, event | category | flops | bytes accessed | tf_op | source)
XLA Modules:
  0.0 127.8 jit_solution(9694029293358723913)
XLA Ops:
  0.0 14.0 %leaf.1 = (bf16[512,512]{1,0:T(8,128)(2,1)}, bf16[512,512]{1,0:T(8,128)(2,1)}, f32[256,128]{1,0:T(8,128)}, f32[512,512]{1,0:T(8,128)}, f32[8,512]{1,0:T(8,128)}) custom-call(f32[3,512]{1,0:T(4,128)} %coord_ref.1, f32[1,512]{1,0:T(1,128)} %bitcast.14, s32[1,512]{1,0:T(1,128)} %bitcast.15, s32[1,512]{1,0:T(1,128)} %order_ref.1, bf16[4,256,512]{2,1,0:T(8,128)(2,1)} %basis_any.1), custom_call_target="tpu_custom_call" | custom-call | tf_op jit(solution)/shard_map/leaf/pallas_call | solution.py:177
  14.0 32.3 %sum_gather.1 = (f32[8,2688]{1,0:T(8,128)}, f32[2,4,4,8,1152]{4,3,2,1,0:T(8,128)}) custom-call(bf16[512,512]{1,0:T(8,128)(2,1)} %get-tuple-element.20.mh_ref, bf16[512,512]{1,0:T(8,128)(2,1)} %get-tuple-element.21.ml_ref, f32[256,128]{1,0:T(8,128)} %get-tuple-element.22.tile_ref, bf16[4,256,512]{2,1,0:T(8,128)(2,1)} %basis_any.1), custom_call_target="tpu_custom_call" | custom-call | tf_op jit(solution)/shard_map/sum_gather/pallas_call | solution.py:520
  46.3 6.3 %inverse.3.inverse_ref = f32[256,256]{1,0:T(8,128)} custom-call(f32[256,1152]{1,0:T(8,128)} %bitcast.7), custom_call_target="tpu_custom_call" | custom-call | tf_op jit(solution)/shard_map/inverse/pallas_call | solution.py:199
  52.6 18.7 %pair_gather1.1 = (f32[8,1664]{1,0:T(8,128)}, f32[2,4,4,8,896]{4,3,2,1,0:T(8,128)}, f32[256,896]{1,0:T(8,128)}) custom-call(f32[256,256]{1,0:T(8,128)} %inverse.3.inverse_ref, f32[256,1152]{1,0:T(8,128)} %bitcast.8, f32[8,2688]{1,0:T(8,128)} %get-tuple-element.24.had_ref), custom_call_target="tpu_custom_call" | custom-call | tf_op jit(solution)/shard_map/pair_gather1/pallas_call | solution.py:565
  71.3 6.1 %inverse.4.inverse_ref = f32[256,256]{1,0:T(8,128)} custom-call(f32[256,896]{1,0:T(8,128)} %bitcast.9), custom_call_target="tpu_custom_call" | custom-call | tf_op jit(solution)/shard_map/inverse/pallas_call | solution.py:199
  77.4 18.0 %pair_gather2.1 = (f32[8,896]{1,0:T(8,128)}, f32[2,4,4,8,640]{4,3,2,1,0:T(8,128)}, f32[256,640]{1,0:T(8,128)}) custom-call(f32[256,256]{1,0:T(8,128)} %inverse.4.inverse_ref, f32[256,896]{1,0:T(8,128)} %bitcast.10, f32[8,1664]{1,0:T(8,128)} %get-tuple-element.26.had_ref), custom_call_target="tpu_custom_call" | custom-call | tf_op jit(solution)/shard_map/pair_gather2/pallas_call | solution.py:565
  95.4 6.1 %inverse.5.inverse_ref = f32[256,256]{1,0:T(8,128)} custom-call(f32[256,640]{1,0:T(8,128)} %bitcast.11), custom_call_target="tpu_custom_call" | custom-call | tf_op jit(solution)/shard_map/inverse/pallas_call | solution.py:199
  101.6 17.5 %pair_gather3.1 = (f32[8,384]{1,0:T(8,128)}, f32[2,4,4,8,384]{4,3,2,1,0:T(8,128)}, f32[256,384]{1,0:T(8,128)}) custom-call(f32[256,256]{1,0:T(8,128)} %inverse.5.inverse_ref, f32[256,640]{1,0:T(8,128)} %bitcast.12, f32[8,896]{1,0:T(8,128)} %get-tuple-element.28.had_ref), custom_call_target="tpu_custom_call" | custom-call | tf_op jit(solution)/shard_map/pair_gather3/pallas_call | solution.py:565
  119.0 8.6 %last.1 = f32[1,512]{1,0:T(1,128)} custom-call(f32[256,384]{1,0:T(8,128)} %bitcast.13, f32[256,896]{1,0:T(8,128)} %get-tuple-element.30.h1_any, f32[256,640]{1,0:T(8,128)} %get-tuple-element.31.h2_any, f32[256,384]{1,0:T(8,128)} %get-tuple-element.32.h3_any, f32[512,512]{1,0:T(8,128)} %get-tuple-element.33.inverse_any, bf16[4,256,512]{2,1,0:T(8,128)(2,1)} %basis_any.1, ...), custom_call_target="tpu_custom_call" | custom-call | tf_op jit(solution)/shard_map/last/pallas_call | solution.py:271

commit v4 on v3

--- a/solution.py
+++ b/solution.py
@@ -69,28 +69,38 @@
     ).astype(F32)
 
 
-def newton_inverse(s, z_ref):
-    n = s.shape[0]
-    bound = jnp.max(jnp.sum(jnp.abs(s), axis=0, keepdims=True))
+def newton_inverses(matrices, z_refs):
+    n = matrices[0].shape[0]
+    sums = [jnp.sum(jnp.abs(s), axis=0, keepdims=True) for s in matrices]
+    bound = jnp.max(functools.reduce(jnp.maximum, sums))
     alpha = 2.0 / (1.0 + bound)
     gap = (bound - 1.0) / (bound + 1.0)
     scale = 2.0 / (2.0 - gap * gap)
-    z_ref[...] = (alpha * scale) * (2.0 * eye(n) - alpha * s)
+    for s, z_ref in zip(matrices, z_refs):
+        z_ref[...] = (alpha * scale) * (2.0 * eye(n) - alpha * s)
     gap = gap * gap / (2.0 - gap * gap)
-    parts = split(s)
+    parts = [split(s) for s in matrices]
 
     def body(gap):
+        scale = 2.0 / (2.0 - gap * gap)
+        for part, z_ref in zip(parts, z_refs):
+            z = z_ref[...]
+            zs = split(z)
+            residual = eye(n) - dot3(part, zs)
+            z_ref[...] = scale * (z + dot3(zs, split(residual)))
+        return gap * gap / (2.0 - gap * gap)
+
+    lax.while_loop(lambda gap: gap > 2e-3, body, gap)
+    found = []
+    for s, z_ref in zip(matrices, z_refs):
         z = z_ref[...]
-        zs = split(z)
-        residual = eye(n) - dot3(parts, zs)
-        scale = 2.0 / (2.0 - gap * gap)
-        z_ref[...] = scale * (z + dot3(zs, split(residual)))
-        return gap * gap / (2.0 - gap * gap)
-
-    lax.while_loop(lambda gap: gap > 2e-3, body, gap)
-    z = z_ref[...]
-    residual = eye(n) - dot_f32(s, z)
-    return z + dot3(split(z), split(residual))
+        residual = eye(n) - dot_f32(s, z)
+        found.append(z + dot3(split(z), split(residual)))
+    return found
+
+
+def newton_inverse(s, z_ref):
+    return newton_inverses([s], [z_ref])[0]
 
 
 def leaf_kernel(coord_ref, latent_ref, label_ref, order_ref, basis_ref, mh_ref, ml_ref, tile_ref,
@@ -153,13 +163,13 @@
             mh_ref[rows, span] = hi
             ml_ref[rows, span] = lo
     solved = row_dot(right_side, split3(inverse_ref[...]))
-    weighted = split3(root_weight * solved)
-    lane = lax.broadcasted_iota(jnp.int32, (LANES, M), 0)
+    weighted = [jnp.broadcast_to(part.astype(F32), (LANES, M)).astype(BF16) for part in split3(root_weight * solved)]
+    bases = basis_ref[...].reshape(LEVELS * R, M)
+    projections = dot(bases, weighted[0], NT) + (dot(bases, weighted[1], NT) + dot(bases, weighted[2], NT))
+    lane = lax.broadcasted_iota(jnp.int32, (R, LANES), 1)
     tile = jnp.zeros((R, LANES), F32)
     for level in range(LEVELS):
-        for piece in weighted:
-            placed = jnp.where(lane == level, piece.astype(F32), 0.0).astype(BF16)
-            tile = tile + dot(basis_ref[level], placed, NT)
+        tile = jnp.where(lane == level, projections[level * R:(level + 1) * R], tile)
     tile_ref[...] = tile
     row = lax.broadcasted_iota(jnp.int32, (8, M), 0)
     rows_ref[...] = jnp.where(row == 0, root_weight, right_side)
@@ -237,45 +247,59 @@
     return LANES + R * (left * (left + 1) // 2)
 
 
-def last_kernel(gathered_ref, h1_any, h2_any, h3_any, inverse_any, basis_any, rows_ref, out_ref,
-                z_ref, h1_ref, h2_ref, h3_ref, inverse_ref, basis_ref, sems):
+NODE = own_width(2)
+
+
+def last_kernel(gathered_ref, h1_any, h2_any, inverse_any, basis_any, rows_ref, out_ref,
+                za_ref, zb_ref, h1_ref, h2_ref, inverse_ref, basis_ref, sems):
     copies = [
         pltpu.make_async_copy(source, target, sems.at[i])
         for i, (source, target) in enumerate(
-            ((h3_any, h3_ref), (h2_any, h2_ref), (h1_any, h1_ref), (inverse_any, inverse_ref), (basis_any, basis_ref))
+            ((h2_any, h2_ref), (h1_any, h1_ref), (inverse_any, inverse_ref), (basis_any, basis_ref))
         )
     ]
     for copy in copies:
         copy.start()
-    inverse = newton_inverse(gathered_ref[:, 0:R] + eye(R), z_ref)
-    h4 = dot3(split(inverse), split(gathered_ref[:, R:R + LANES]))
+    inverses = newton_inverses(
+        [gathered_ref[:, q * NODE:q * NODE + R] + eye(R) for q in range(2)], [za_ref, zb_ref]
+    )
+    core, right, h3 = eye(R), jnp.zeros((1, R), F32), None
+    for q in range(2):
+        at = q * NODE
+        coupling = gathered_ref[:, at + R:at + 2 * R]
+        h = dot3(split(inverses[q]), split(gathered_ref[:, at + R:at + 2 * R + LANES]))
+        drop = dot3(split(coupling.T), split(h))
+        core = core + (gathered_ref[:, at + 2 * R + LANES:at + NODE] - drop[:, 0:R])
+        right = right + (gathered_ref[:, at + 2 * R:at + 2 * R + LANES].T[3:4, :] - drop[:, R:].T[2:3, :])
+        h3 = h if h3 is None else h3
+    z = row_dot(right, split(newton_inverse(core, za_ref)))
     for copy in copies:
         copy.wait()
-    h_refs = (h1_ref, h2_ref, h3_ref)
-    rows = [h_refs[i][:, (3 - i) * R:(3 - i) * R + LANES].T[i:i + 1, :] for i in range(3)] + [h4.T[3:4, :]]
+    h_all = (h1_ref[...], h2_ref[...], h3)
+    rows = [h[:, (3 - i) * R:(3 - i) * R + LANES].T[i:i + 1, :] for i, h in enumerate(h_all)] + [z]
     total = jnp.zeros((16, M), F32)
     for level in reversed(range(LEVELS)):
         z = packed_rows(rows[level])
         total = total + dot(z, basis_ref[level])
         for i in range(level):
             at = (level - i - 1) * R
-            parts = split(h_refs[i][:, at:at + R])
+            parts = split(h_all[i][:, at:at + R])
             drop = dot(z, parts[0], NT) + dot(z, parts[1], NT)
             rows[i] = rows[i] - ((drop[0:1] + drop[1:2]) + drop[2:3])
     spread = (total[0:1] + total[1:2]) + total[2:3]
     out_ref[...] = row_dot(rows_ref[1:2] - rows_ref[0:1] * spread, split3(inverse_ref[...]))
 
 
-def last_call(gathered, h1, h2, h3, inverse, rows, bases):
-    kept = (h1, h2, h3, inverse, bases)
+def last_call(gathered, h1, h2, inverse, rows, bases):
+    kept = (h1, h2, inverse, bases)
     return pl.pallas_call(
         last_kernel,
         out_shape=jax.ShapeDtypeStruct((1, M), F32),
-        in_specs=vmem(1) + [pl.BlockSpec(memory_space=pl.ANY)] * 5 + vmem(1),
+        in_specs=vmem(1) + [pl.BlockSpec(memory_space=pl.ANY)] * 4 + vmem(1),
         out_specs=vmem(1)[0],
-        scratch_shapes=[pltpu.VMEM((R, R), F32)]
+        scratch_shapes=[pltpu.VMEM((R, R), F32)] * 2
         + [pltpu.VMEM(array.shape, array.dtype) for array in kept]
-        + [pltpu.SemaphoreType.DMA((5,))],
+        + [pltpu.SemaphoreType.DMA((4,))],
         compiler_params=PARAMS,
         name="last",
     )(gathered, *kept, rows)
@@ -535,17 +559,12 @@
     )(mh, ml, tile, bases)
 
 
-def pair_kernel(level, inverse_ref, before_ref, had_ref, own_ref, gathered_ref, h_ref, part_ref, got_ref,
+def pair_kernel(inverse_ref, before_ref, had_ref, own_ref, gathered_ref, h_ref, part_ref, got_ref,
                 send_sem, recv_sem, gather_send, gather_recv):
     plane, x, y, core = place()
-    step = 2 ** (level - 1)
-    if level == LEVELS - 1:
-        beyond = 2 * step - 1 - plane
-    else:
-        beyond = plane + step - 2 * step * (plane // step % 2)
-    mates = plane_mates() + [device(beyond, x, y, core)]
+    mates = plane_mates() + [device(plane + 1 - 2 * (plane % 2), x, y, core)]
     greet(mates)
-    eliminate(LEVELS - level + 1, inverse_ref, before_ref, had_ref, part_ref, h_ref)
+    eliminate(LEVELS, inverse_ref, before_ref, had_ref, part_ref, h_ref)
     meet(mates)
     swap = send(part_ref, got_ref, (send_sem, recv_sem), 0, mates[-1])
     swap.wait_recv()
@@ -558,12 +577,12 @@
     swap.wait_send()
 
 
-def pair_call(level, inverse, gathered, own):
-    left = LEVELS - level
+def pair_call(inverse, gathered, own):
+    left = LEVELS - 1
     width = left * R + LANES
     slab = (8, own_width(left))
     return pl.pallas_call(
-        functools.partial(pair_kernel, level),
+        pair_kernel,
         out_shape=(
             jax.ShapeDtypeStruct(slab, F32),
             jax.ShapeDtypeStruct((2,) + TILES + (width,), F32),
@@ -580,9 +599,58 @@
             pltpu.SemaphoreType.DMA((GATHER_COPIES,)),
         ],
         compiler_params=pltpu.CompilerParams(
-            vmem_limit_bytes=60 * 1024 * 1024, collective_id=level, has_side_effects=True
+            vmem_limit_bytes=60 * 1024 * 1024, collective_id=1, has_side_effects=True
         ),
-        name=f"pair_gather{level}",
+        name="pair_gather",
+    )(inverse, gathered, own)
+
+
+def node_kernel(inverse_ref, before_ref, had_ref, gathered_ref, h_ref, part_ref, got_ref, both_ref,
+                send_sem, recv_sem, gather_send, gather_recv):
+    plane, x, y, core = place()
+    odd = plane // 2 % 2
+    planes = (plane + 2 - 4 * odd, (plane + 6 + 4 * odd) % 8, (plane + 5 - 2 * (plane % 2)) % 8)
+    others = [device(other, x, y, core) for other in planes]
+    mates = plane_mates() + others
+    greet(mates)
+    eliminate(LEVELS - 1, inverse_ref, before_ref, had_ref, part_ref, h_ref)
+    meet(mates)
+    swaps = [send(part_ref, got_ref.at[i], (send_sem, recv_sem), i, others[i]) for i in (2, 0, 1)]
+    for swap in swaps:
+        swap.wait_recv()
+    both_ref[:, 0:NODE] = part_ref[...] + got_ref[0]
+    both_ref[:, NODE:] = got_ref[1] + got_ref[2]
+    gather = Gather(both_ref, gathered_ref, (gather_send, gather_recv))
+    gather.start()
+    gather.turn()
+    gather.finish()
+    gather.close()
+    for swap in swaps:
+        swap.wait_send()
+
+
+def node_call(inverse, gathered, own):
+    return pl.pallas_call(
+        node_kernel,
+        out_shape=(
+            jax.ShapeDtypeStruct((2,) + TILES + (2 * NODE,), F32),
+            jax.ShapeDtypeStruct((R, 2 * R + LANES), F32),
+        ),
+        in_specs=vmem(3),
+        out_specs=tuple(vmem(2)),
+        scratch_shapes=[
+            pltpu.VMEM((8, NODE), F32),
+            pltpu.VMEM((3, 8, NODE), F32),
+            pltpu.VMEM((8, 2 * NODE), F32),
+            pltpu.SemaphoreType.DMA((3,)),
+            pltpu.SemaphoreType.DMA((3,)),
+            pltpu.SemaphoreType.DMA((GATHER_COPIES,)),
+            pltpu.SemaphoreType.DMA((GATHER_COPIES,)),
+        ],
+        compiler_params=pltpu.CompilerParams(
+            vmem_limit_bytes=60 * 1024 * 1024, collective_id=2, has_side_effects=True
+        ),
+        name="node_gather",
     )(inverse, gathered, own)
 
 
@@ -592,12 +660,10 @@
     )
     own, gathered = sum_call(mh, ml, tile, level_bases)
     gathered = gathered.reshape(R, HEAD)
-    h = []
-    for level in range(1, LEVELS):
-        own, after, part = pair_call(level, inverse_call(gathered), gathered, own)
-        h.append(part)
-        gathered = after.reshape(R, (LEVELS - level) * R + LANES)
-    return last_call(gathered, *h, inverse, rows, level_bases).reshape(M)
+    own, after, h1 = pair_call(inverse_call(gathered), gathered, own)
+    gathered = after.reshape(R, 3 * R + LANES)
+    both, h2 = node_call(inverse_call(gathered), gathered, own)
+    return last_call(both.reshape(R, 2 * NODE), h1, h2, inverse, rows, level_bases).reshape(M)
 
 
 def solution(mesh):

time: 128 us -> 118 us (0.922)
  Pallas kernels: 128 us -> 117 us
    pallas_call x3 -> x2, Pallas kernels: 54.2 us -> 42.7 us  [the longest x1 24.5 us: node_call(): pl.pallas_call(node_kernel, out_shape=(jax.ShapeDtypeStruct((2,) + TILES...]
    pallas_call x1, Pallas kernels: 8.6 us -> 16.6 us  [last_call(): pl.pallas_call(last_kernel, out_shape=jax.ShapeDtypeStruct((1, M), F32),...]
    pallas_call x3 -> x2, Pallas kernels: 18.5 us -> 12.4 us  [inverse_call(): pl.pallas_call(inverse_kernel, grid=(1,), out_shape=jax.ShapeDtypeStruct(...]
where the time goes in v4:
time: 118 us; the launch traced here: 117 us
  Pallas kernels  117 us (99%)
    pallas_call x1, Pallas kernels, sum_call(): pl.pallas_call(sum_kernel, out_shape=(jax.ShapeDtypeStruct((8, FRONT), F3...  32.3 us
    pallas_call x1, Pallas kernels, node_call(): pl.pallas_call(node_kernel, out_shape=(jax.ShapeDtypeStruct((2,) + TILES...  24.5 us
    pallas_call x1, Pallas kernels, pair_call(): pl.pallas_call(pair_kernel, out_shape=(jax.ShapeDtypeStruct(slab, F32), j...  18.2 us
    pallas_call x1, Pallas kernels, last_call(): pl.pallas_call(last_kernel, out_shape=jax.ShapeDtypeStruct((1, M), F32),...  16.6 us
    pallas_call x1, Pallas kernels, leaf_call(): pl.pallas_call(leaf_kernel, out_shape=(jax.ShapeDtypeStruct((M, M), BF16)...  13.3 us
    pallas_call x2, Pallas kernels, inverse_call(): pl.pallas_call(inverse_kernel, grid=(1,), out_shape=jax.ShapeDtypeStruct(...  12.4 us

profile of v4, /device:TPU:1, one launch (start us, length us, event | category | flops | bytes accessed | tf_op | source)
XLA Modules:
  0.0 117.5 jit_solution(16528732881994445651)
XLA Ops:
  0.0 13.3 %leaf.1 = (bf16[512,512]{1,0:T(8,128)(2,1)}, bf16[512,512]{1,0:T(8,128)(2,1)}, f32[256,128]{1,0:T(8,128)}, f32[512,512]{1,0:T(8,128)}, f32[8,512]{1,0:T(8,128)}) custom-call(f32[3,512]{1,0:T(4,128)} %coord_ref.1, f32[1,512]{1,0:T(1,128)} %bitcast.11, s32[1,512]{1,0:T(1,128)} %bitcast.12, s32[1,512]{1,0:T(1,128)} %order_ref.1, bf16[4,256,512]{2,1,0:T(8,128)(2,1)} %basis_any.1), custom_call_target="tpu_custom_call" | custom-call | tf_op jit(solution)/shard_map/leaf/pallas_call | solution.py:187
  13.3 32.3 %sum_gather.1 = (f32[8,2688]{1,0:T(8,128)}, f32[2,4,4,8,1152]{4,3,2,1,0:T(8,128)}) custom-call(bf16[512,512]{1,0:T(8,128)(2,1)} %get-tuple-element.17.mh_ref, bf16[512,512]{1,0:T(8,128)(2,1)} %get-tuple-element.18.ml_ref, f32[256,128]{1,0:T(8,128)} %get-tuple-element.19.tile_ref, bf16[4,256,512]{2,1,0:T(8,128)(2,1)} %basis_any.1), custom_call_target="tpu_custom_call" | custom-call | tf_op jit(solution)/shard_map/sum_gather/pallas_call | solution.py:544
  45.6 6.3 %inverse.2.inverse_ref = f32[256,256]{1,0:T(8,128)} custom-call(f32[256,1152]{1,0:T(8,128)} %bitcast.6), custom_call_target="tpu_custom_call" | custom-call | tf_op jit(solution)/shard_map/inverse/pallas_call | solution.py:209
  51.9 18.2 %pair_gather.1 = (f32[8,1664]{1,0:T(8,128)}, f32[2,4,4,8,896]{4,3,2,1,0:T(8,128)}, f32[256,896]{1,0:T(8,128)}) custom-call(f32[256,256]{1,0:T(8,128)} %inverse.2.inverse_ref, f32[256,1152]{1,0:T(8,128)} %bitcast.7, f32[8,2688]{1,0:T(8,128)} %get-tuple-element.21.had_ref), custom_call_target="tpu_custom_call" | custom-call | tf_op jit(solution)/shard_map/pair_gather/pallas_call | solution.py:584
  70.1 6.1 %inverse.3.inverse_ref = f32[256,256]{1,0:T(8,128)} custom-call(f32[256,896]{1,0:T(8,128)} %bitcast.8), custom_call_target="tpu_custom_call" | custom-call | tf_op jit(solution)/shard_map/inverse/pallas_call | solution.py:209
  76.2 24.5 %node_gather.1 = (f32[2,4,4,8,1792]{4,3,2,1,0:T(8,128)}, f32[256,640]{1,0:T(8,128)}) custom-call(f32[256,256]{1,0:T(8,128)} %inverse.3.inverse_ref, f32[256,896]{1,0:T(8,128)} %bitcast.9, f32[8,1664]{1,0:T(8,128)} %get-tuple-element.23.had_ref), custom_call_target="tpu_custom_call" | custom-call | tf_op jit(solution)/shard_map/node_gather/pallas_call | solution.py:633
  100.7 16.6 %last.1 = f32[1,512]{1,0:T(1,128)} custom-call(f32[256,1792]{1,0:T(8,128)} %bitcast.10, f32[256,896]{1,0:T(8,128)} %get-tuple-element.25.h1_any, f32[256,640]{1,0:T(8,128)} %get-tuple-element.26.h2_any, f32[512,512]{1,0:T(8,128)} %get-tuple-element.27.inverse_any, bf16[4,256,512]{2,1,0:T(8,128)(2,1)} %basis_any.1, f32[8,512]{1,0:T(8,128)} %get-tuple-element.28.rows_ref), custom_call_target="tpu_custom_call" | custom-call | tf_op jit(solution)/shard_map/last/pallas_call | solution.py:295

commit v5 on v4

--- a/solution.py
+++ b/solution.py
@@ -69,38 +69,51 @@
     ).astype(F32)
 
 
-def newton_inverses(matrices, z_refs):
+def newton_polish(s, z):
+    residual = eye(s.shape[0]) - dot_f32(s, z)
+    return z + dot3(split(z), split(residual))
+
+
+def newton_rough(matrices, refs):
     n = matrices[0].shape[0]
     sums = [jnp.sum(jnp.abs(s), axis=0, keepdims=True) for s in matrices]
     bound = jnp.max(functools.reduce(jnp.maximum, sums))
     alpha = 2.0 / (1.0 + bound)
     gap = (bound - 1.0) / (bound + 1.0)
     scale = 2.0 / (2.0 - gap * gap)
-    for s, z_ref in zip(matrices, z_refs):
-        z_ref[...] = (alpha * scale) * (2.0 * eye(n) - alpha * s)
-    gap = gap * gap / (2.0 - gap * gap)
-    parts = [split(s) for s in matrices]
+    for s, ref in zip(matrices, refs):
+        first = eye(n) - alpha * s
+        parts = split(first)
+        ref[0:n] = (alpha * scale) * (eye(n) + first)
+        ref[n:] = (1.0 - scale) * eye(n) + scale * dot3(parts, parts)
 
     def body(gap):
         scale = 2.0 / (2.0 - gap * gap)
-        for part, z_ref in zip(parts, z_refs):
-            z = z_ref[...]
-            zs = split(z)
-            residual = eye(n) - dot3(part, zs)
-            z_ref[...] = scale * (z + dot3(zs, split(residual)))
+        for ref in refs:
+            hi, lo = split(ref[...])
+            product = dot3((hi, lo), (hi[n:], lo[n:]))
+            ref[0:n] = scale * (ref[0:n] + product[0:n])
+            ref[n:] = (1.0 - scale) * eye(n) + scale * product[n:]
         return gap * gap / (2.0 - gap * gap)
 
-    lax.while_loop(lambda gap: gap > 2e-3, body, gap)
-    found = []
-    for s, z_ref in zip(matrices, z_refs):
-        z = z_ref[...]
-        residual = eye(n) - dot_f32(s, z)
-        found.append(z + dot3(split(z), split(residual)))
-    return found
-
-
-def newton_inverse(s, z_ref):
-    return newton_inverses([s], [z_ref])[0]
+    lax.while_loop(lambda gap: gap > 2e-3, body, gap * gap / (2.0 - gap * gap))
+
+    def polish(step, carry):
+        for s, ref in zip(matrices, refs):
+            ref[0:n] = newton_polish(s, ref[0:n])
+        return carry
+
+    extra = jnp.where(bound < 256.0, 0, jnp.where(bound < 8192.0, 1, 2))
+    lax.fori_loop(0, extra, polish, 0)
+
+
+def newton_inverses(matrices, refs):
+    newton_rough(matrices, refs)
+    return [newton_polish(s, ref[0:s.shape[0]]) for s, ref in zip(matrices, refs)]
+
+
+def newton_inverse(s, ref):
+    return newton_inverses([s], [ref])[0]
 
 
 def leaf_kernel(coord_ref, latent_ref, label_ref, order_ref, basis_ref, mh_ref, ml_ref, tile_ref,
@@ -150,11 +163,12 @@
     u = dot_f32(x, a_ref[top, bottom])
     v = dot_f32(a_ref[bottom, top], x)
     schur = newton_inverse(a_ref[bottom, bottom] - dot_f32(v, a_ref[top, bottom]), z_ref)
-    us = dot_f32(u, schur)
+    schur_parts, v_parts = split(schur), split(v)
+    us = dot3(split(u), schur_parts)
     inverse_ref[bottom, bottom] = schur
     inverse_ref[top, bottom] = -us
-    inverse_ref[bottom, top] = -dot_f32(schur, v)
-    inverse_ref[top, top] = x + dot_f32(us, v)
+    inverse_ref[bottom, top] = -dot3(schur_parts, v_parts)
+    inverse_ref[top, top] = x + dot3(split(us), v_parts)
 
     for i in range(4):
         for j in range(4):
@@ -195,14 +209,15 @@
         ),
         in_specs=vmem(5),
         out_specs=tuple(vmem(5)),
-        scratch_shapes=[pltpu.VMEM((M, M), F32), pltpu.VMEM((R, R), F32)],
+        scratch_shapes=[pltpu.VMEM((M, M), F32), pltpu.VMEM((2 * R, R), F32)],
         compiler_params=PARAMS,
         name="leaf",
     )(coords, latent, labels, order, bases)
 
 
 def inverse_kernel(gathered_ref, inverse_ref, z_ref):
-    inverse_ref[...] = newton_inverse(gathered_ref[...] + eye(R), z_ref)
+    newton_rough([gathered_ref[...] + eye(R)], [z_ref])
+    inverse_ref[...] = z_ref[0:R]
 
 
 def inverse_call(gathered):
@@ -212,14 +227,15 @@
         out_shape=jax.ShapeDtypeStruct((R, R), F32),
         in_specs=[pl.BlockSpec((R, R), lambda i: (0, 0))],
         out_specs=pl.BlockSpec((R, R), lambda i: (0, 0)),
-        scratch_shapes=[pltpu.VMEM((R, R), F32)],
+        scratch_shapes=[pltpu.VMEM((2 * R, R), F32)],
         compiler_params=PARAMS,
         name="inverse",
     )(gathered)
 
 
 def eliminate(left, inverse_ref, gathered_ref, own_ref, next_ref, h_ref):
-    h = dot3(split(inverse_ref[...]), split(gathered_ref[:, R:left * R + LANES]))
+    inverse = newton_polish(gathered_ref[:, 0:R] + eye(R), inverse_ref[...])
+    h = dot3(split(inverse), split(gathered_ref[:, R:left * R + LANES]))
     h_ref[...] = h
     width = (left - 1) * R
     h_parts = split(h)
@@ -248,6 +264,8 @@
 
 
 NODE = own_width(2)
+BOTH_B = 2 * R + LANES
+BOTH = 5 * R + LANES
 
 
 def last_kernel(gathered_ref, h1_any, h2_any, inverse_any, basis_any, rows_ref, out_ref,
@@ -260,23 +278,27 @@
     ]
     for copy in copies:
         copy.start()
-    inverses = newton_inverses(
-        [gathered_ref[:, q * NODE:q * NODE + R] + eye(R) for q in range(2)], [za_ref, zb_ref]
-    )
-    core, right, h3 = eye(R), jnp.zeros((1, R), F32), None
-    for q in range(2):
-        at = q * NODE
+    starts = (0, BOTH_B)
+    inverses = newton_inverses([gathered_ref[:, at:at + R] + eye(R) for at in starts], [za_ref, zb_ref])
+    tile = gathered_ref[:, 2 * R:BOTH_B]
+    tile_parts = split(tile)
+    core = eye(R) + gathered_ref[:, BOTH_B + 2 * R:]
+    right = tile.T[3:4, :]
+    kept = []
+    for at, inverse, lane in zip(starts, inverses, (2, 1)):
         coupling = gathered_ref[:, at + R:at + 2 * R]
-        h = dot3(split(inverses[q]), split(gathered_ref[:, at + R:at + 2 * R + LANES]))
-        drop = dot3(split(coupling.T), split(h))
-        core = core + (gathered_ref[:, at + 2 * R + LANES:at + NODE] - drop[:, 0:R])
-        right = right + (gathered_ref[:, at + 2 * R:at + 2 * R + LANES].T[3:4, :] - drop[:, R:].T[2:3, :])
-        h3 = h if h3 is None else h3
+        inverse_parts, turned = split(inverse), split(coupling.T)
+        h = dot3(inverse_parts, split(coupling))
+        tile_h = dot3(inverse_parts, tile_parts)
+        core = core - dot3(turned, split(h))
+        right = right - dot3(turned, split(tile_h)).T[lane:lane + 1, :]
+        kept.append((h, tile_h))
     z = row_dot(right, split(newton_inverse(core, za_ref)))
     for copy in copies:
         copy.wait()
-    h_all = (h1_ref[...], h2_ref[...], h3)
-    rows = [h[:, (3 - i) * R:(3 - i) * R + LANES].T[i:i + 1, :] for i, h in enumerate(h_all)] + [z]
+    h_all = (h1_ref[...], h2_ref[...], kept[0][0])
+    tiles = (h1_ref[:, 3 * R:], h2_ref[:, 2 * R:], kept[0][1])
+    rows = [part.T[i:i + 1, :] for i, part in enumerate(tiles)] + [z]
     total = jnp.zeros((16, M), F32)
     for level in reversed(range(LEVELS)):
         z = packed_rows(rows[level])
@@ -297,7 +319,7 @@
         out_shape=jax.ShapeDtypeStruct((1, M), F32),
         in_specs=vmem(1) + [pl.BlockSpec(memory_space=pl.ANY)] * 4 + vmem(1),
         out_specs=vmem(1)[0],
-        scratch_shapes=[pltpu.VMEM((R, R), F32)] * 2
+        scratch_shapes=[pltpu.VMEM((2 * R, R), F32)] * 2
         + [pltpu.VMEM(array.shape, array.dtype) for array in kept]
         + [pltpu.SemaphoreType.DMA((4,))],
         compiler_params=PARAMS,
@@ -367,7 +389,7 @@
         self.own, self.out, self.sems = own_ref, gathered_ref, sems
         self.halves = ((0, slice(0, half)), (1, slice(half, width)))
         self.width, self.index, self.fence = width, 0, []
-        self.first, self.second = [], []
+        self.first, self.second = [], ({}, {})
 
     def send(self, source, target, to):
         self.index += 1
@@ -376,46 +398,47 @@
     def share(self, block):
         self.fence.append(self.send(block, block, partner()))
 
+    def tile(self, axis, back):
+        plane, x, y, core = place()
+        at = along(axis, 4 - back)[1]
+        return (core, at, y) if axis == 0 else (core, x, at)
+
     def start(self):
         plane, x, y, core = place()
-        for axis, cols in self.halves:
-            self.first.append([
-                self.send(self.own.at[:, cols], self.out.at[core, x, y, :, cols], along(axis, k)[0])
-                for k in (2, 1, 3)
-            ])
+        for half, (axis, cols) in enumerate(self.halves):
+            block = self.own.at[:, cols]
+            target = self.out.at[core, x, y, :, cols]
+            self.first.append({k: self.send(block, target, along(axis, k)[0]) for k in (2, 1, 3)})
+            self.second[half][0] = {k: self.send(block, target, along(1 - axis, k)[0]) for k in (2, 1, 3)}
         whole = slice(0, self.width)
         self.fence.append(self.send(self.own.at[:, whole], self.out.at[core, x, y], partner()))
         self.out[core, x, y] = self.own[:, whole]
 
     def turn(self):
-        plane, x, y, core = place()
-        for (axis, cols), copies in zip(self.halves, self.first):
-            for copy in copies:
-                copy.wait_recv()
-            if axis == 0:
-                block = self.out.at[core, :, y, :, cols]
-            else:
-                block = self.out.at[core, x, :, :, cols]
-            self.second.append([self.send(block, block, along(1 - axis, k)[0]) for k in (2, 1, 3)])
-        for axis, cols in self.halves:
-            for k in (1, 2, 3):
-                at = (along(axis, k)[1], y) if axis == 0 else (x, along(axis, k)[1])
-                self.share(self.out.at[core, at[0], at[1], :, cols])
+        for back in (1, 3, 2):
+            for half, (axis, cols) in enumerate(self.halves):
+                self.first[half][back].wait_recv()
+                core, at_x, at_y = self.tile(axis, back)
+                block = self.out.at[core, at_x, at_y, :, cols]
+                self.second[half][back] = {k: self.send(block, block, along(1 - axis, k)[0]) for k in (2, 1, 3)}
+                self.share(block)
 
     def finish(self):
         plane, x, y, core = place()
-        for i, k in ((1, 1), (2, 3), (0, 2)):
-            for (axis, cols), moved in zip(self.halves, self.second):
-                moved[i].wait_recv()
+        for k in (1, 3, 2):
+            for half, (axis, cols) in enumerate(self.halves):
+                for back in (0, 1, 3, 2):
+                    self.second[half][back][k].wait_recv()
                 if axis == 0:
                     self.share(self.out.at[core, :, along(1, 4 - k)[1], :, cols])
                 else:
                     self.share(self.out.at[core, along(0, 4 - k)[1], :, :, cols])
 
     def close(self):
-        for copies in self.first + self.second:
-            for copy in copies:
-                copy.wait_send()
+        for half in range(2):
+            for copies in [self.first[half], *self.second[half].values()]:
+                for copy in copies.values():
+                    copy.wait_send()
         for copy in self.fence:
             copy.wait()
 
@@ -477,7 +500,7 @@
             copy.wait_send()
 
 
-GATHER_COPIES = 25
+GATHER_COPIES = 43
 HEAD = LEVELS * R + LANES
 TAIL = FRONT - HEAD
 HEAD_CUT = 5 * LANES
@@ -618,8 +641,15 @@
     swaps = [send(part_ref, got_ref.at[i], (send_sem, recv_sem), i, others[i]) for i in (2, 0, 1)]
     for swap in swaps:
         swap.wait_recv()
-    both_ref[:, 0:NODE] = part_ref[...] + got_ref[0]
-    both_ref[:, NODE:] = got_ref[1] + got_ref[2]
+    mine = part_ref[...] + got_ref[0]
+    other = got_ref[1] + got_ref[2]
+    lane = lax.broadcasted_iota(jnp.int32, (8, LANES), 1)
+    tile, other_tile = mine[:, 2 * R:BOTH_B], other[:, 2 * R:BOTH_B]
+    tile = jnp.where(lane == 1, other_tile[:, 2:3], jnp.where(lane == 3, tile + other_tile, tile))
+    both_ref[:, 0:2 * R] = mine[:, 0:2 * R]
+    both_ref[:, 2 * R:BOTH_B] = tile
+    both_ref[:, BOTH_B:BOTH_B + 2 * R] = other[:, 0:2 * R]
+    both_ref[:, BOTH_B + 2 * R:] = mine[:, BOTH_B:] + other[:, BOTH_B:]
     gather = Gather(both_ref, gathered_ref, (gather_send, gather_recv))
     gather.start()
     gather.turn()
@@ -633,7 +663,7 @@
     return pl.pallas_call(
         node_kernel,
         out_shape=(
-            jax.ShapeDtypeStruct((2,) + TILES + (2 * NODE,), F32),
+            jax.ShapeDtypeStruct((2,) + TILES + (BOTH,), F32),
             jax.ShapeDtypeStruct((R, 2 * R + LANES), F32),
         ),
         in_specs=vmem(3),
@@ -641,7 +671,7 @@
         scratch_shapes=[
             pltpu.VMEM((8, NODE), F32),
             pltpu.VMEM((3, 8, NODE), F32),
-            pltpu.VMEM((8, 2 * NODE), F32),
+            pltpu.VMEM((8, BOTH), F32),
             pltpu.SemaphoreType.DMA((3,)),
             pltpu.SemaphoreType.DMA((3,)),
             pltpu.SemaphoreType.DMA((GATHER_COPIES,)),
@@ -663,7 +693,7 @@
     own, after, h1 = pair_call(inverse_call(gathered), gathered, own)
     gathered = after.reshape(R, 3 * R + LANES)
     both, h2 = node_call(inverse_call(gathered), gathered, own)
-    return last_call(both.reshape(R, 2 * NODE), h1, h2, inverse, rows, level_bases).reshape(M)
+    return last_call(both.reshape(R, BOTH), h1, h2, inverse, rows, level_bases).reshape(M)
 
 
 def solution(mesh):

time: 118 us -> 110 us (0.932)
  Pallas kernels: 117 us -> 110 us
    pallas_call x2, Pallas kernels: 12.4 us -> 8.46 us  [inverse_call(): pl.pallas_call(inverse_kernel, grid=(1,), out_shape=jax.ShapeDtypeStruct(...]
    pallas_call x1, Pallas kernels: 13.3 us -> 11 us  [leaf_call(): pl.pallas_call(leaf_kernel, out_shape=(jax.ShapeDtypeStruct((M, M), BF16)...]
    pallas_call x1, Pallas kernels: 16.6 us -> 14.6 us  [last_call(): pl.pallas_call(last_kernel, out_shape=jax.ShapeDtypeStruct((1, M), F32),...]
where the time goes in v5:
time: 110 us
  Pallas kernels  110 us (100%)
    pallas_call x1, Pallas kernels, sum_call(): pl.pallas_call(sum_kernel, out_shape=(jax.ShapeDtypeStruct((8, FRONT), F3...  32.5 us
    pallas_call x1, Pallas kernels, node_call(): pl.pallas_call(node_kernel, out_shape=(jax.ShapeDtypeStruct((2,) + TILES...  24.3 us
    pallas_call x1, Pallas kernels, pair_call(): pl.pallas_call(pair_kernel, out_shape=(jax.ShapeDtypeStruct(slab, F32), j...  18.8 us
    pallas_call x1, Pallas kernels, last_call(): pl.pallas_call(last_kernel, out_shape=jax.ShapeDtypeStruct((1, M), F32),...  14.6 us
    pallas_call x1, Pallas kernels, leaf_call(): pl.pallas_call(leaf_kernel, out_shape=(jax.ShapeDtypeStruct((M, M), BF16)...  11 us
    pallas_call x2, Pallas kernels, inverse_call(): pl.pallas_call(inverse_kernel, grid=(1,), out_shape=jax.ShapeDtypeStruct(...  8.46 us

profile of v5, /device:TPU:1, one launch (start us, length us, event | category | flops | bytes accessed | tf_op | source)
XLA Modules:
  0.0 109.7 jit_solution(427884155203139761)
XLA Ops:
  0.0 11.0 %leaf.1 = (bf16[512,512]{1,0:T(8,128)(2,1)}, bf16[512,512]{1,0:T(8,128)(2,1)}, f32[256,128]{1,0:T(8,128)}, f32[512,512]{1,0:T(8,128)}, f32[8,512]{1,0:T(8,128)}) custom-call(f32[3,512]{1,0:T(4,128)} %coord_ref.1, f32[1,512]{1,0:T(1,128)} %bitcast.11, s32[1,512]{1,0:T(1,128)} %bitcast.12, s32[1,512]{1,0:T(1,128)} %order_ref.1, bf16[4,256,512]{2,1,0:T(8,128)(2,1)} %basis_any.1), custom_call_target="tpu_custom_call" | custom-call | tf_op jit(solution)/shard_map/leaf/pallas_call | solution.py:201
  11.0 32.5 %sum_gather.1 = (f32[8,2688]{1,0:T(8,128)}, f32[2,4,4,8,1152]{4,3,2,1,0:T(8,128)}) custom-call(bf16[512,512]{1,0:T(8,128)(2,1)} %get-tuple-element.17.mh_ref, bf16[512,512]{1,0:T(8,128)(2,1)} %get-tuple-element.18.ml_ref, f32[256,128]{1,0:T(8,128)} %get-tuple-element.19.tile_ref, bf16[4,256,512]{2,1,0:T(8,128)(2,1)} %basis_any.1), custom_call_target="tpu_custom_call" | custom-call | tf_op jit(solution)/shard_map/sum_gather/pallas_call | solution.py:567
  43.5 4.3 %inverse.2.inverse_ref = f32[256,256]{1,0:T(8,128)} custom-call(f32[256,1152]{1,0:T(8,128)} %bitcast.6), custom_call_target="tpu_custom_call" | custom-call | tf_op jit(solution)/shard_map/inverse/pallas_call | solution.py:224
  47.8 18.8 %pair_gather.1 = (f32[8,1664]{1,0:T(8,128)}, f32[2,4,4,8,896]{4,3,2,1,0:T(8,128)}, f32[256,896]{1,0:T(8,128)}) custom-call(f32[256,256]{1,0:T(8,128)} %inverse.2.inverse_ref, f32[256,1152]{1,0:T(8,128)} %bitcast.7, f32[8,2688]{1,0:T(8,128)} %get-tuple-element.21.had_ref), custom_call_target="tpu_custom_call" | custom-call | tf_op jit(solution)/shard_map/pair_gather/pallas_call | solution.py:607
  66.6 4.1 %inverse.3.inverse_ref = f32[256,256]{1,0:T(8,128)} custom-call(f32[256,896]{1,0:T(8,128)} %bitcast.8), custom_call_target="tpu_custom_call" | custom-call | tf_op jit(solution)/shard_map/inverse/pallas_call | solution.py:224
  70.7 24.3 %node_gather.1 = (f32[2,4,4,8,1408]{4,3,2,1,0:T(8,128)}, f32[256,640]{1,0:T(8,128)}) custom-call(f32[256,256]{1,0:T(8,128)} %inverse.3.inverse_ref, f32[256,896]{1,0:T(8,128)} %bitcast.9, f32[8,1664]{1,0:T(8,128)} %get-tuple-element.23.had_ref), custom_call_target="tpu_custom_call" | custom-call | tf_op jit(solution)/shard_map/node_gather/pallas_call | solution.py:663
  95.0 14.6 %last.1 = f32[1,512]{1,0:T(1,128)} custom-call(f32[256,1408]{1,0:T(8,128)} %bitcast.10, f32[256,896]{1,0:T(8,128)} %get-tuple-element.25.h1_any, f32[256,640]{1,0:T(8,128)} %get-tuple-element.26.h2_any, f32[512,512]{1,0:T(8,128)} %get-tuple-element.27.inverse_any, bf16[4,256,512]{2,1,0:T(8,128)(2,1)} %basis_any.1, f32[8,512]{1,0:T(8,128)} %get-tuple-element.28.rows_ref), custom_call_target="tpu_custom_call" | custom-call | tf_op jit(solution)/shard_map/last/pallas_call | solution.py:317

commit v6 on v5

--- a/solution.py
+++ b/solution.py
@@ -116,16 +116,15 @@
     return newton_inverses([s], [ref])[0]
 
 
-def leaf_kernel(coord_ref, latent_ref, label_ref, order_ref, basis_ref, mh_ref, ml_ref, tile_ref,
-                inverse_ref, rows_ref, a_ref, z_ref):
-    picked = lax.broadcasted_iota(jnp.int32, (M, M), 0) == order_ref[...]
+def leaf_kernel(sites_ref, mh_ref, ml_ref, inverse_ref, rows_ref, a_ref, z_ref):
+    picked = lax.broadcasted_iota(jnp.int32, (M, M), 0) == sites_ref[5:6].astype(jnp.int32)
     one_hot = jnp.where(picked, 1.0, 0.0).astype(BF16)
-    hi, mid, lo = split3(latent_ref[...])
+    hi, mid, lo = split3(sites_ref[3:4])
     row = lax.broadcasted_iota(jnp.int32, (16, M), 0)
     packed = jnp.where(row == 0, hi.astype(F32), 0.0)
     packed = jnp.where(row == 1, mid.astype(F32), packed)
     packed = jnp.where(row == 2, lo.astype(F32), packed)
-    packed = jnp.where(row == 3, label_ref[...].astype(F32), packed)
+    packed = jnp.where(row == 3, sites_ref[4:5], packed)
     got = dot(packed.astype(BF16), one_hot)
     tree_latent = (got[0:1] + got[1:2]) + got[2:3]
     tree_target = got[3:4]
@@ -137,7 +136,7 @@
     def column(value, i):
         return jnp.broadcast_to(value[:, i * LANES:(i + 1) * LANES], (LANES, LANES)).T
 
-    axes = [coord_ref[k:k + 1, :] for k in range(3)]
+    axes = [sites_ref[k:k + 1, :] for k in range(3)]
     columns = []
     for i in range(4):
         cols = [column(axis, i) for axis in axes]
@@ -177,16 +176,8 @@
             mh_ref[rows, span] = hi
             ml_ref[rows, span] = lo
     solved = row_dot(right_side, split3(inverse_ref[...]))
-    weighted = [jnp.broadcast_to(part.astype(F32), (LANES, M)).astype(BF16) for part in split3(root_weight * solved)]
-    bases = basis_ref[...].reshape(LEVELS * R, M)
-    projections = dot(bases, weighted[0], NT) + (dot(bases, weighted[1], NT) + dot(bases, weighted[2], NT))
-    lane = lax.broadcasted_iota(jnp.int32, (R, LANES), 1)
-    tile = jnp.zeros((R, LANES), F32)
-    for level in range(LEVELS):
-        tile = jnp.where(lane == level, projections[level * R:(level + 1) * R], tile)
-    tile_ref[...] = tile
     row = lax.broadcasted_iota(jnp.int32, (8, M), 0)
-    rows_ref[...] = jnp.where(row == 0, root_weight, right_side)
+    rows_ref[...] = jnp.where(row == 0, root_weight, jnp.where(row == 1, right_side, root_weight * solved))
 
 
 def vmem(n):
@@ -194,25 +185,24 @@
 
 
 FRONT = LEVELS * R + LANES + 6 * R
-PARAMS = pltpu.CompilerParams(vmem_limit_bytes=60 * 1024 * 1024)
-
-
-def leaf_call(coords, latent, labels, order, bases):
+PARAMS = pltpu.CompilerParams(vmem_limit_bytes=20 * 1024 * 1024)
+
+
+def leaf_call(sites):
     return pl.pallas_call(
         leaf_kernel,
         out_shape=(
             jax.ShapeDtypeStruct((M, M), BF16),
             jax.ShapeDtypeStruct((M, M), BF16),
-            jax.ShapeDtypeStruct((R, LANES), F32),
             jax.ShapeDtypeStruct((M, M), F32),
             jax.ShapeDtypeStruct((8, M), F32),
         ),
-        in_specs=vmem(5),
-        out_specs=tuple(vmem(5)),
+        in_specs=vmem(1),
+        out_specs=tuple(vmem(4)),
         scratch_shapes=[pltpu.VMEM((M, M), F32), pltpu.VMEM((2 * R, R), F32)],
         compiler_params=PARAMS,
         name="leaf",
-    )(coords, latent, labels, order, bases)
+    )(sites)
 
 
 def inverse_kernel(gathered_ref, inverse_ref, z_ref):
@@ -268,16 +258,7 @@
 BOTH = 5 * R + LANES
 
 
-def last_kernel(gathered_ref, h1_any, h2_any, inverse_any, basis_any, rows_ref, out_ref,
-                za_ref, zb_ref, h1_ref, h2_ref, inverse_ref, basis_ref, sems):
-    copies = [
-        pltpu.make_async_copy(source, target, sems.at[i])
-        for i, (source, target) in enumerate(
-            ((h2_any, h2_ref), (h1_any, h1_ref), (inverse_any, inverse_ref), (basis_any, basis_ref))
-        )
-    ]
-    for copy in copies:
-        copy.start()
+def last_kernel(gathered_ref, h1_ref, h2_ref, inverse_ref, basis_ref, rows_ref, out_ref, za_ref, zb_ref):
     starts = (0, BOTH_B)
     inverses = newton_inverses([gathered_ref[:, at:at + R] + eye(R) for at in starts], [za_ref, zb_ref])
     tile = gathered_ref[:, 2 * R:BOTH_B]
@@ -294,8 +275,6 @@
         right = right - dot3(turned, split(tile_h)).T[lane:lane + 1, :]
         kept.append((h, tile_h))
     z = row_dot(right, split(newton_inverse(core, za_ref)))
-    for copy in copies:
-        copy.wait()
     h_all = (h1_ref[...], h2_ref[...], kept[0][0])
     tiles = (h1_ref[:, 3 * R:], h2_ref[:, 2 * R:], kept[0][1])
     rows = [part.T[i:i + 1, :] for i, part in enumerate(tiles)] + [z]
@@ -313,18 +292,15 @@
 
 
 def last_call(gathered, h1, h2, inverse, rows, bases):
-    kept = (h1, h2, inverse, bases)
     return pl.pallas_call(
         last_kernel,
         out_shape=jax.ShapeDtypeStruct((1, M), F32),
-        in_specs=vmem(1) + [pl.BlockSpec(memory_space=pl.ANY)] * 4 + vmem(1),
+        in_specs=vmem(6),
         out_specs=vmem(1)[0],
-        scratch_shapes=[pltpu.VMEM((2 * R, R), F32)] * 2
-        + [pltpu.VMEM(array.shape, array.dtype) for array in kept]
-        + [pltpu.SemaphoreType.DMA((4,))],
+        scratch_shapes=[pltpu.VMEM((2 * R, R), F32)] * 2,
         compiler_params=PARAMS,
         name="last",
-    )(gathered, *kept, rows)
+    )(gathered, h1, h2, inverse, bases, rows)
 
 
 def place():
@@ -517,7 +493,7 @@
     return [pltpu.VMEM(shape, F32) for shape in shapes] + [pltpu.SemaphoreType.DMA((14,))] * 2
 
 
-def sum_kernel(mh_ref, ml_ref, tile_ref, basis_ref, own_ref, gathered_ref, *scratch):
+def sum_kernel(mh_ref, ml_ref, rows_ref, basis_ref, own_ref, gathered_ref, tile_ref, *scratch):
     plane, x, y, core = place()
     mates = plane_mates()
     greet(mates)
@@ -542,6 +518,14 @@
     head_sum = Scatter(*scratch[1:11], scratch[11:13])
     tail_sum = Scatter(*scratch[14:24], scratch[24:26])
     gather = Gather(own_ref, gathered_ref, scratch[26:28])
+    weighted = [jnp.broadcast_to(part.astype(F32), (LANES, M)).astype(BF16) for part in split3(rows_ref[2:3])]
+    bases = basis_ref[...].reshape(LEVELS * R, M)
+    projections = dot(bases, weighted[0], NT) + (dot(bases, weighted[1], NT) + dot(bases, weighted[2], NT))
+    lane = lax.broadcasted_iota(jnp.int32, (R, LANES), 1)
+    tile = jnp.zeros((R, LANES), F32)
+    for level in range(LEVELS):
+        tile = jnp.where(lane == level, projections[level * R:(level + 1) * R], tile)
+    tile_ref[...] = tile
     grams(1 - core, 0, theirs0, 0)
     meet(mates)
     head_sum.swap(theirs0)
@@ -563,7 +547,7 @@
     tail_sum.close()
 
 
-def sum_call(mh, ml, tile, bases):
+def sum_call(mh, ml, rows, bases):
     return pl.pallas_call(
         sum_kernel,
         out_shape=(
@@ -572,14 +556,15 @@
         ),
         in_specs=vmem(4),
         out_specs=tuple(vmem(2)),
-        scratch_shapes=scatter_scratch(HEAD, HEAD_CUT)
+        scratch_shapes=[pltpu.VMEM((R, LANES), F32)]
+        + scatter_scratch(HEAD, HEAD_CUT)
         + scatter_scratch(TAIL, TAIL_CUT)
         + [pltpu.SemaphoreType.DMA((GATHER_COPIES,))] * 2,
         compiler_params=pltpu.CompilerParams(
-            vmem_limit_bytes=60 * 1024 * 1024, collective_id=0, has_side_effects=True
+            vmem_limit_bytes=20 * 1024 * 1024, collective_id=0, has_side_effects=True
         ),
         name="sum_gather",
-    )(mh, ml, tile, bases)
+    )(mh, ml, rows, bases)
 
 
 def pair_kernel(inverse_ref, before_ref, had_ref, own_ref, gathered_ref, h_ref, part_ref, got_ref,
@@ -622,7 +607,7 @@
             pltpu.SemaphoreType.DMA((GATHER_COPIES,)),
         ],
         compiler_params=pltpu.CompilerParams(
-            vmem_limit_bytes=60 * 1024 * 1024, collective_id=1, has_side_effects=True
+            vmem_limit_bytes=20 * 1024 * 1024, collective_id=1, has_side_effects=True
         ),
         name="pair_gather",
     )(inverse, gathered, own)
@@ -678,17 +663,18 @@
             pltpu.SemaphoreType.DMA((GATHER_COPIES,)),
         ],
         compiler_params=pltpu.CompilerParams(
-            vmem_limit_bytes=60 * 1024 * 1024, collective_id=2, has_side_effects=True
+            vmem_limit_bytes=20 * 1024 * 1024, collective_id=2, has_side_effects=True
         ),
         name="node_gather",
     )(inverse, gathered, own)
 
 
 def local(coords, latent, labels, site_order, level_bases):
-    mh, ml, tile, inverse, rows = leaf_call(
-        coords, latent.reshape(1, M), labels.reshape(1, M), site_order, level_bases
+    sites = jnp.concatenate(
+        [coords, latent.reshape(1, M), labels.reshape(1, M).astype(F32), site_order.astype(F32)], axis=0
     )
-    own, gathered = sum_call(mh, ml, tile, level_bases)
+    mh, ml, inverse, rows = leaf_call(sites)
+    own, gathered = sum_call(mh, ml, rows, level_bases)
     gathered = gathered.reshape(R, HEAD)
     own, after, h1 = pair_call(inverse_call(gathered), gathered, own)
     gathered = after.reshape(R, 3 * R + LANES)

time: 110 us -> 98.8 us (0.90)
  Pallas kernels: 110 us -> 95.5 us
  other arithmetic: 0 us -> 2.09 us
  local copies, waits for them, and re-layouts: 0 us -> 1.24 us
    pallas_call x2, Pallas kernels: 8.46 us -> 5.14 us  [inverse_call(): pl.pallas_call(inverse_kernel, grid=(1,), out_shape=jax.ShapeDtypeStruct(...]
    pallas_call x1, Pallas kernels: 11 us -> 8.12 us  [leaf_call(): pl.pallas_call(leaf_kernel, out_shape=(jax.ShapeDtypeStruct((M, M), BF16)...]
    pallas_call x1, Pallas kernels: 32.5 us -> 29.9 us  [sum_call(): pl.pallas_call(sum_kernel, out_shape=(jax.ShapeDtypeStruct((8, FRONT), F3...]
    pallas_call x1, Pallas kernels: 18.8 us -> 16.6 us  [pair_call(): pl.pallas_call(pair_kernel, out_shape=(jax.ShapeDtypeStruct(slab, F32), j...]
    pallas_call x1, Pallas kernels: 24.3 us -> 22.7 us  [node_call(): pl.pallas_call(node_kernel, out_shape=(jax.ShapeDtypeStruct((2,) + TILES...]
    pallas_call x1, Pallas kernels: 14.6 us -> 13.1 us  [last_call(): pl.pallas_call(last_kernel, out_shape=jax.ShapeDtypeStruct((1, M), F32),...]
    convert_element_type x0 -> x2, other arithmetic: none -> 1.37 us  [the longest x1 0.68 us: local(): site_order.astype(F32)]
    unnamed x0 -> x4, local copies, waits for them, and re-layouts: none -> 1.24 us
where the time goes in v6:
time: 98.8 us; the launch traced here: 98.9 us
  Pallas kernels  95.5 us (97%)
  other arithmetic  2.09 us (2%)
  local copies, waits for them, and re-layouts  1.24 us (1%)
    pallas_call x1, Pallas kernels, sum_call(): pl.pallas_call(sum_kernel, out_shape=(jax.ShapeDtypeStruct((8, FRONT), F3...  29.9 us
    pallas_call x1, Pallas kernels, node_call(): pl.pallas_call(node_kernel, out_shape=(jax.ShapeDtypeStruct((2,) + TILES...  22.7 us
    pallas_call x1, Pallas kernels, pair_call(): pl.pallas_call(pair_kernel, out_shape=(jax.ShapeDtypeStruct(slab, F32), j...  16.6 us
    pallas_call x1, Pallas kernels, last_call(): pl.pallas_call(last_kernel, out_shape=jax.ShapeDtypeStruct((1, M), F32),...  13.1 us
    pallas_call x1, Pallas kernels, leaf_call(): pl.pallas_call(leaf_kernel, out_shape=(jax.ShapeDtypeStruct((M, M), BF16)...  8.12 us
    pallas_call x2, Pallas kernels, inverse_call(): pl.pallas_call(inverse_kernel, grid=(1,), out_shape=jax.ShapeDtypeStruct(...  5.14 us

profile of v6, /device:TPU:1, one launch (start us, length us, event | category | flops | bytes accessed | tf_op | source)
XLA Modules:
  0.0 98.9 jit_solution(11822641129826191700)
XLA Ops:
  0.0 0.7 convert_element_type.9
  0.7 0.7 convert_element_type.11
  1.4 0.7 pad_maximum_fusion.sites_ref
  2.1 8.1 %leaf.1 = (bf16[512,512]{1,0:T(8,128)(2,1)S(1)}, bf16[512,512]{1,0:T(8,128)(2,1)S(1)}, f32[512,512]{1,0:T(8,128)S(1)}, f32[8,512]{1,0:T(8,128)S(1)}) custom-call(f32[6,512]{1,0:T(8,128)S(1)} %pad_maximum_fusion.sites_ref), custom_call_target="tpu_custom_call" | custom-call | tf_op jit(solution)/shard_map/leaf/pallas_call | solution.py:192
  10.2 0.0 copy-start
  10.2 1.2 %copy-done = bf16[4,256,512]{2,1,0:T(8,128)(2,1)S(1)} copy-done((bf16[4,256,512]{2,1,0:T(8,128)(2,1)S(1)}, bf16[4,256,512]{2,1,0:T(8,128)(2,1)}, u32[]{:S(2)}) %copy-start) | copy-done | bytes 1048600
  11.5 29.9 %sum_gather.1 = (f32[8,2688]{1,0:T(8,128)S(1)}, f32[2,4,4,8,1152]{4,3,2,1,0:T(8,128)S(1)}) custom-call(bf16[512,512]{1,0:T(8,128)(2,1)S(1)} %get-tuple-element.16.mh_ref, bf16[512,512]{1,0:T(8,128)(2,1)S(1)} %get-tuple-element.17.ml_ref, f32[8,512]{1,0:T(8,128)S(1)} %get-tuple-element.18.rows_ref, bf16[4,256,512]{2,1,0:T(8,128)(2,1)S(1)} %copy-done), custom_call_target="tpu_custom_call" | custom-call | tf_op jit(solution)/shard_map/sum_gather/pallas_call | solution.py:551
  41.4 2.7 %inverse.2.inverse_ref = f32[256,256]{1,0:T(8,128)S(1)} custom-call(f32[256,1152]{1,0:T(8,128)S(1)} %bitcast.6), custom_call_target="tpu_custom_call" | custom-call | tf_op jit(solution)/shard_map/inverse/pallas_call | solution.py:214
  44.0 16.6 %pair_gather.1 = (f32[8,1664]{1,0:T(8,128)S(1)}, f32[2,4,4,8,896]{4,3,2,1,0:T(8,128)S(1)}, f32[256,896]{1,0:T(8,128)S(1)}) custom-call(f32[256,256]{1,0:T(8,128)S(1)} %inverse.2.inverse_ref, f32[256,1152]{1,0:T(8,128)S(1)} %bitcast.7, f32[8,2688]{1,0:T(8,128)S(1)} %get-tuple-element.20.had_ref), custom_call_target="tpu_custom_call" | custom-call | tf_op jit(solution)/shard_map/pair_gather/pallas_call | solution.py:592
  60.6 0.0 copy-start.1
  60.6 2.5 %inverse.3.inverse_ref = f32[256,256]{1,0:T(8,128)S(1)} custom-call(f32[256,896]{1,0:T(8,128)S(1)} %bitcast.8), custom_call_target="tpu_custom_call" | custom-call | tf_op jit(solution)/shard_map/inverse/pallas_call | solution.py:214
  63.1 22.7 %node_gather.1 = (f32[2,4,4,8,1408]{4,3,2,1,0:T(8,128)S(1)}, f32[256,640]{1,0:T(8,128)S(1)}) custom-call(f32[256,256]{1,0:T(8,128)S(1)} %inverse.3.inverse_ref, f32[256,896]{1,0:T(8,128)S(1)} %bitcast.9, f32[8,1664]{1,0:T(8,128)S(1)} %get-tuple-element.22.had_ref), custom_call_target="tpu_custom_call" | custom-call | tf_op jit(solution)/shard_map/node_gather/pallas_call | solution.py:648
  85.8 0.0 copy-done.1
  85.8 13.1 %last.1 = f32[1,512]{1,0:T(1,128)} custom-call(f32[256,1408]{1,0:T(8,128)S(1)} %bitcast.10, f32[256,896]{1,0:T(8,128)S(1)} %get-tuple-element.24.h1_ref, f32[256,640]{1,0:T(8,128)S(1)} %get-tuple-element.25.h2_ref, f32[512,512]{1,0:T(8,128)S(1)} %get-tuple-element.26.inverse_ref, bf16[4,256,512]{2,1,0:T(8,128)(2,1)S(1)} %copy-done.1, ...), custom_call_target="tpu_custom_call" | custom-call | tf_op jit(solution)/shard_map/last/pallas_call | solution.py:295
Async XLA Ops:
  10.2 1.2 %copy-start = (bf16[4,256,512]{2,1,0:T(8,128)(2,1)S(1)}, bf16[4,256,512]{2,1,0:T(8,128)(2,1)}, u32[]{:S(2)}) copy-start(bf16[4,256,512]{2,1,0:T(8,128)(2,1)} %basis_ref.3) | copy-start | bytes 3145732
  60.6 25.2 %copy-start.1 = (bf16[4,256,512]{2,1,0:T(8,128)(2,1)S(1)}, bf16[4,256,512]{2,1,0:T(8,128)(2,1)}, u32[]{:S(2)}) copy-start(bf16[4,256,512]{2,1,0:T(8,128)(2,1)} %basis_ref.3) | copy-start | bytes 3145732

commit v7 on v6

--- a/solution.py
+++ b/solution.py
@@ -116,15 +116,15 @@
     return newton_inverses([s], [ref])[0]
 
 
-def leaf_kernel(sites_ref, mh_ref, ml_ref, inverse_ref, rows_ref, a_ref, z_ref):
-    picked = lax.broadcasted_iota(jnp.int32, (M, M), 0) == sites_ref[5:6].astype(jnp.int32)
+def leaf_kernel(sites_ref, marks_ref, mh_ref, ml_ref, inverse_ref, rows_ref, a_ref, z_ref):
+    picked = lax.broadcasted_iota(jnp.int32, (M, M), 0) == marks_ref[1:2]
     one_hot = jnp.where(picked, 1.0, 0.0).astype(BF16)
     hi, mid, lo = split3(sites_ref[3:4])
     row = lax.broadcasted_iota(jnp.int32, (16, M), 0)
     packed = jnp.where(row == 0, hi.astype(F32), 0.0)
     packed = jnp.where(row == 1, mid.astype(F32), packed)
     packed = jnp.where(row == 2, lo.astype(F32), packed)
-    packed = jnp.where(row == 3, sites_ref[4:5], packed)
+    packed = jnp.where(row == 3, marks_ref[0:1].astype(F32), packed)
     got = dot(packed.astype(BF16), one_hot)
     tree_latent = (got[0:1] + got[1:2]) + got[2:3]
     tree_target = got[3:4]
@@ -188,7 +188,7 @@
 PARAMS = pltpu.CompilerParams(vmem_limit_bytes=20 * 1024 * 1024)
 
 
-def leaf_call(sites):
+def leaf_call(sites, marks):
     return pl.pallas_call(
         leaf_kernel,
         out_shape=(
@@ -197,12 +197,13 @@
             jax.ShapeDtypeStruct((M, M), F32),
             jax.ShapeDtypeStruct((8, M), F32),
         ),
-        in_specs=vmem(1),
+        in_specs=vmem(2),
         out_specs=tuple(vmem(4)),
         scratch_shapes=[pltpu.VMEM((M, M), F32), pltpu.VMEM((2 * R, R), F32)],
         compiler_params=PARAMS,
+        cost_estimate=pl.CostEstimate(flops=8_000_000_000, bytes_accessed=3_000_000, transcendentals=1_000_000),
         name="leaf",
-    )(sites)
+    )(sites, marks)
 
 
 def inverse_kernel(gathered_ref, inverse_ref, z_ref):
@@ -288,7 +289,7 @@
             drop = dot(z, parts[0], NT) + dot(z, parts[1], NT)
             rows[i] = rows[i] - ((drop[0:1] + drop[1:2]) + drop[2:3])
     spread = (total[0:1] + total[1:2]) + total[2:3]
-    out_ref[...] = row_dot(rows_ref[1:2] - rows_ref[0:1] * spread, split3(inverse_ref[...]))
+    out_ref[...] = row_dot(rows_ref[1:2] - rows_ref[0:1] * spread, split(inverse_ref[...]))
 
 
 def last_call(gathered, h1, h2, inverse, rows, bases):
@@ -574,15 +575,22 @@
     greet(mates)
     eliminate(LEVELS, inverse_ref, before_ref, had_ref, part_ref, h_ref)
     meet(mates)
-    swap = send(part_ref, got_ref, (send_sem, recv_sem), 0, mates[-1])
-    swap.wait_recv()
-    own_ref[...] = part_ref[...] + got_ref[...]
+    cut = gathered_ref.shape[-1]
+    pieces = (slice(0, cut), slice(cut, part_ref.shape[-1]))
+    swaps = [
+        send(part_ref.at[:, cols], got_ref.at[:, cols], (send_sem, recv_sem), i, mates[-1]) for i, cols in enumerate(pieces)
+    ]
+    swaps[0].wait_recv()
+    own_ref[:, 0:cut] = part_ref[:, 0:cut] + got_ref[:, 0:cut]
     gather = Gather(own_ref, gathered_ref, (gather_send, gather_recv))
     gather.start()
     gather.turn()
+    swaps[1].wait_recv()
+    own_ref[:, cut:] = part_ref[:, cut:] + got_ref[:, cut:]
     gather.finish()
     gather.close()
-    swap.wait_send()
+    for swap in swaps:
+        swap.wait_send()
 
 
 def pair_call(inverse, gathered, own):
@@ -601,8 +609,8 @@
         scratch_shapes=[
             pltpu.VMEM(slab, F32),
             pltpu.VMEM(slab, F32),
-            pltpu.SemaphoreType.DMA((1,)),
-            pltpu.SemaphoreType.DMA((1,)),
+            pltpu.SemaphoreType.DMA((2,)),
+            pltpu.SemaphoreType.DMA((2,)),
             pltpu.SemaphoreType.DMA((GATHER_COPIES,)),
             pltpu.SemaphoreType.DMA((GATHER_COPIES,)),
         ],
@@ -670,10 +678,9 @@
 
 
 def local(coords, latent, labels, site_order, level_bases):
-    sites = jnp.concatenate(
-        [coords, latent.reshape(1, M), labels.reshape(1, M).astype(F32), site_order.astype(F32)], axis=0
-    )
-    mh, ml, inverse, rows = leaf_call(sites)
+    sites = jnp.concatenate([coords, latent.reshape(1, M)], axis=0)
+    marks = jnp.concatenate([labels.reshape(1, M), site_order], axis=0)
+    mh, ml, inverse, rows = leaf_call(sites, marks)
     own, gathered = sum_call(mh, ml, rows, level_bases)
     gathered = gathered.reshape(R, HEAD)
     own, after, h1 = pair_call(inverse_call(gathered), gathered, own)

time: 98.8 us -> 97.2 us (0.984); the launches traced: 98.9 us -> 96.1 us
  local copies, waits for them, and re-layouts: 1.24 us -> 0.01 us
    convert_element_type x2 -> x0, other arithmetic: 1.37 us -> none  [the longest x1 0.68 us: local(): site_order.astype(F32)]
    unnamed x4 -> x2, local copies, waits for them, and re-layouts: 1.24 us -> 0.01 us
where the time goes in v7:
time: 97.2 us; the launch traced here: 96.1 us
  Pallas kernels  94.6 us (97%)
  other arithmetic  1.43 us (1%)
    pallas_call x1, Pallas kernels, sum_call(): pl.pallas_call(sum_kernel, out_shape=(jax.ShapeDtypeStruct((8, FRONT), F3...  30.2 us
    pallas_call x1, Pallas kernels, node_call(): pl.pallas_call(node_kernel, out_shape=(jax.ShapeDtypeStruct((2,) + TILES...  21.7 us
    pallas_call x1, Pallas kernels, pair_call(): pl.pallas_call(pair_kernel, out_shape=(jax.ShapeDtypeStruct(slab, F32), j...  16.5 us
    pallas_call x1, Pallas kernels, last_call(): pl.pallas_call(last_kernel, out_shape=jax.ShapeDtypeStruct((1, M), F32),...  13 us
    pallas_call x1, Pallas kernels, leaf_call(): pl.pallas_call(leaf_kernel, out_shape=(jax.ShapeDtypeStruct((M, M), BF16)...  8.12 us
    pallas_call x2, Pallas kernels, inverse_call(): pl.pallas_call(inverse_kernel, grid=(1,), out_shape=jax.ShapeDtypeStruct(...  5.14 us

profile of v7, /device:TPU:1, one launch (start us, length us, event | category | flops | bytes accessed | tf_op | source)
XLA Modules:
  0.0 96.1 jit_solution(7331697381433008786)
XLA Ops:
  0.0 0.7 pad_add_fusion.marks_ref
  0.7 0.7 pad_maximum_fusion.sites_ref
  1.4 0.0 copy-start
  1.4 8.1 %leaf.1 = (bf16[512,512]{1,0:T(8,128)(2,1)S(1)}, bf16[512,512]{1,0:T(8,128)(2,1)S(1)}, f32[512,512]{1,0:T(8,128)S(1)}, f32[8,512]{1,0:T(8,128)S(1)}) custom-call(f32[4,512]{1,0:T(4,128)S(1)} %pad_maximum_fusion.sites_ref, s32[2,512]{1,0:T(2,128)S(1)} %pad_add_fusion.marks_ref), custom_call_target="tpu_custom_call" | custom-call | flops 8000000000 | bytes 3000000 | tf_op jit(solution)/shard_map/leaf/pallas_call | solution.py:192
  9.5 0.0 copy-done
  9.6 30.2 %sum_gather.1 = (f32[8,2688]{1,0:T(8,128)S(1)}, f32[2,4,4,8,1152]{4,3,2,1,0:T(8,128)S(1)}) custom-call(bf16[512,512]{1,0:T(8,128)(2,1)S(1)} %get-tuple-element.16.mh_ref, bf16[512,512]{1,0:T(8,128)(2,1)S(1)} %get-tuple-element.17.ml_ref, f32[8,512]{1,0:T(8,128)S(1)} %get-tuple-element.18.rows_ref, bf16[4,256,512]{2,1,0:T(8,128)(2,1)S(1)} %copy-done), custom_call_target="tpu_custom_call" | custom-call | tf_op jit(solution)/shard_map/sum_gather/pallas_call | solution.py:552
  39.8 2.7 %inverse.2.inverse_ref = f32[256,256]{1,0:T(8,128)S(1)} custom-call(f32[256,1152]{1,0:T(8,128)S(1)} %bitcast.6), custom_call_target="tpu_custom_call" | custom-call | tf_op jit(solution)/shard_map/inverse/pallas_call | solution.py:215
  42.5 16.5 %pair_gather.1 = (f32[8,1664]{1,0:T(8,128)S(1)}, f32[2,4,4,8,896]{4,3,2,1,0:T(8,128)S(1)}, f32[256,896]{1,0:T(8,128)S(1)}) custom-call(f32[256,256]{1,0:T(8,128)S(1)} %inverse.2.inverse_ref, f32[256,1152]{1,0:T(8,128)S(1)} %bitcast.7, f32[8,2688]{1,0:T(8,128)S(1)} %get-tuple-element.20.had_ref), custom_call_target="tpu_custom_call" | custom-call | tf_op jit(solution)/shard_map/pair_gather/pallas_call | solution.py:600
  58.9 2.5 %inverse.3.inverse_ref = f32[256,256]{1,0:T(8,128)S(1)} custom-call(f32[256,896]{1,0:T(8,128)S(1)} %bitcast.8), custom_call_target="tpu_custom_call" | custom-call | tf_op jit(solution)/shard_map/inverse/pallas_call | solution.py:215
  61.4 21.7 %node_gather.1 = (f32[2,4,4,8,1408]{4,3,2,1,0:T(8,128)S(1)}, f32[256,640]{1,0:T(8,128)S(1)}) custom-call(f32[256,256]{1,0:T(8,128)S(1)} %inverse.3.inverse_ref, f32[256,896]{1,0:T(8,128)S(1)} %bitcast.9, f32[8,1664]{1,0:T(8,128)S(1)} %get-tuple-element.22.had_ref), custom_call_target="tpu_custom_call" | custom-call | tf_op jit(solution)/shard_map/node_gather/pallas_call | solution.py:656
  83.2 13.0 %last.1 = f32[1,512]{1,0:T(1,128)} custom-call(f32[256,1408]{1,0:T(8,128)S(1)} %bitcast.10, f32[256,896]{1,0:T(8,128)S(1)} %get-tuple-element.24.h1_ref, f32[256,640]{1,0:T(8,128)S(1)} %get-tuple-element.25.h2_ref, f32[512,512]{1,0:T(8,128)S(1)} %get-tuple-element.26.inverse_ref, bf16[4,256,512]{2,1,0:T(8,128)(2,1)S(1)} %copy-done, ...), custom_call_target="tpu_custom_call" | custom-call | tf_op jit(solution)/shard_map/last/pallas_call | solution.py:296
Async XLA Ops:
  1.4 8.1 %copy-start = (bf16[4,256,512]{2,1,0:T(8,128)(2,1)S(1)}, bf16[4,256,512]{2,1,0:T(8,128)(2,1)}, u32[]{:S(2)}) copy-start(bf16[4,256,512]{2,1,0:T(8,128)(2,1)} %basis_ref.3) | copy-start | bytes 3145732

commit v8 on v7

--- a/solution.py
+++ b/solution.py
@@ -539,8 +539,8 @@
     tail_sum.first()
     head_sum.finish(own_ref, 0)
     gather.start()
+    tail_sum.second()
     gather.turn()
-    tail_sum.second()
     gather.finish()
     tail_sum.finish(own_ref, HEAD)
     gather.close()

time: 97.2 us -> 98 us (level); the launches traced: 96.1 us -> 98.1 us
  Pallas kernels: 94.6 us -> 96.6 us
    pallas_call x1, Pallas kernels: 13 us -> 14.6 us  [last_call(): pl.pallas_call(last_kernel, out_shape=jax.ShapeDtypeStruct((1, M), F32),...]
where the time goes in v8:
time: 98 us; the launch traced here: 98.1 us
  Pallas kernels  96.6 us (99%)
  other arithmetic  1.43 us (1%)
    pallas_call x1, Pallas kernels, sum_call(): pl.pallas_call(sum_kernel, out_shape=(jax.ShapeDtypeStruct((8, FRONT), F3...  30.2 us
    pallas_call x1, Pallas kernels, node_call(): pl.pallas_call(node_kernel, out_shape=(jax.ShapeDtypeStruct((2,) + TILES...  22.2 us
    pallas_call x1, Pallas kernels, pair_call(): pl.pallas_call(pair_kernel, out_shape=(jax.ShapeDtypeStruct(slab, F32), j...  16.4 us
    pallas_call x1, Pallas kernels, last_call(): pl.pallas_call(last_kernel, out_shape=jax.ShapeDtypeStruct((1, M), F32),...  14.6 us
    pallas_call x1, Pallas kernels, leaf_call(): pl.pallas_call(leaf_kernel, out_shape=(jax.ShapeDtypeStruct((M, M), BF16)...  8.12 us
    pallas_call x2, Pallas kernels, inverse_call(): pl.pallas_call(inverse_kernel, grid=(1,), out_shape=jax.ShapeDtypeStruct(...  5.14 us

profile of v8, /device:TPU:1, one launch (start us, length us, event | category | flops | bytes accessed | tf_op | source)
XLA Modules:
  0.0 98.1 jit_solution(17801592817282444405)
XLA Ops:
  0.0 0.7 pad_add_fusion.marks_ref
  0.7 0.7 pad_maximum_fusion.sites_ref
  1.4 0.0 copy-start
  1.4 8.1 %leaf.1 = (bf16[512,512]{1,0:T(8,128)(2,1)S(1)}, bf16[512,512]{1,0:T(8,128)(2,1)S(1)}, f32[512,512]{1,0:T(8,128)S(1)}, f32[8,512]{1,0:T(8,128)S(1)}) custom-call(f32[4,512]{1,0:T(4,128)S(1)} %pad_maximum_fusion.sites_ref, s32[2,512]{1,0:T(2,128)S(1)} %pad_add_fusion.marks_ref), custom_call_target="tpu_custom_call" | custom-call | flops 8000000000 | bytes 3000000 | tf_op jit(solution)/shard_map/leaf/pallas_call | solution.py:192
  9.5 0.0 copy-done
  9.6 30.2 %sum_gather.1 = (f32[8,2688]{1,0:T(8,128)S(1)}, f32[2,4,4,8,1152]{4,3,2,1,0:T(8,128)S(1)}) custom-call(bf16[512,512]{1,0:T(8,128)(2,1)S(1)} %get-tuple-element.16.mh_ref, bf16[512,512]{1,0:T(8,128)(2,1)S(1)} %get-tuple-element.17.ml_ref, f32[8,512]{1,0:T(8,128)S(1)} %get-tuple-element.18.rows_ref, bf16[4,256,512]{2,1,0:T(8,128)(2,1)S(1)} %copy-done), custom_call_target="tpu_custom_call" | custom-call | tf_op jit(solution)/shard_map/sum_gather/pallas_call | solution.py:552
  39.8 2.7 %inverse.2.inverse_ref = f32[256,256]{1,0:T(8,128)S(1)} custom-call(f32[256,1152]{1,0:T(8,128)S(1)} %bitcast.6), custom_call_target="tpu_custom_call" | custom-call | tf_op jit(solution)/shard_map/inverse/pallas_call | solution.py:215
  42.5 16.4 %pair_gather.1 = (f32[8,1664]{1,0:T(8,128)S(1)}, f32[2,4,4,8,896]{4,3,2,1,0:T(8,128)S(1)}, f32[256,896]{1,0:T(8,128)S(1)}) custom-call(f32[256,256]{1,0:T(8,128)S(1)} %inverse.2.inverse_ref, f32[256,1152]{1,0:T(8,128)S(1)} %bitcast.7, f32[8,2688]{1,0:T(8,128)S(1)} %get-tuple-element.20.had_ref), custom_call_target="tpu_custom_call" | custom-call | tf_op jit(solution)/shard_map/pair_gather/pallas_call | solution.py:600
  58.8 2.5 %inverse.3.inverse_ref = f32[256,256]{1,0:T(8,128)S(1)} custom-call(f32[256,896]{1,0:T(8,128)S(1)} %bitcast.8), custom_call_target="tpu_custom_call" | custom-call | tf_op jit(solution)/shard_map/inverse/pallas_call | solution.py:215
  61.3 22.2 %node_gather.1 = (f32[2,4,4,8,1408]{4,3,2,1,0:T(8,128)S(1)}, f32[256,640]{1,0:T(8,128)S(1)}) custom-call(f32[256,256]{1,0:T(8,128)S(1)} %inverse.3.inverse_ref, f32[256,896]{1,0:T(8,128)S(1)} %bitcast.9, f32[8,1664]{1,0:T(8,128)S(1)} %get-tuple-element.22.had_ref), custom_call_target="tpu_custom_call" | custom-call | tf_op jit(solution)/shard_map/node_gather/pallas_call | solution.py:656
  83.5 14.6 %last.1 = f32[1,512]{1,0:T(1,128)} custom-call(f32[256,1408]{1,0:T(8,128)S(1)} %bitcast.10, f32[256,896]{1,0:T(8,128)S(1)} %get-tuple-element.24.h1_ref, f32[256,640]{1,0:T(8,128)S(1)} %get-tuple-element.25.h2_ref, f32[512,512]{1,0:T(8,128)S(1)} %get-tuple-element.26.inverse_ref, bf16[4,256,512]{2,1,0:T(8,128)(2,1)S(1)} %copy-done, ...), custom_call_target="tpu_custom_call" | custom-call | tf_op jit(solution)/shard_map/last/pallas_call | solution.py:296
Async XLA Ops:
  1.4 8.1 %copy-start = (bf16[4,256,512]{2,1,0:T(8,128)(2,1)S(1)}, bf16[4,256,512]{2,1,0:T(8,128)(2,1)}, u32[]{:S(2)}) copy-start(bf16[4,256,512]{2,1,0:T(8,128)(2,1)} %basis_ref.3) | copy-start | bytes 3145732
